TPU v7x, 128 devices: a whole 4x4x4 slice. The times are simulated.
128 devices in a mesh: slab: 16 (over y, x), gore: 8 (over z, core).
Axes of the slice: x: 4, y: 4, z: 4, core: 2. Of those that a mesh axis runs over, the one named last changes fastest.
Arguments:
- fluid_velocity: float32 [3, 128, 256, 1024], P(None, 'slab', 'gore'), may hold values from -6 to 6
- viscosity: float32 [128, 256, 1024], P('slab', 'gore'), may hold values from 0.03 to 0.16
- pressure_jump: float32 [1024, 1024], P('slab', 'gore'), may hold values from -6 to 6
- normals: float32 [3, 1024, 1024], P(None, 'slab', 'gore'), may hold values from -6 to 6
- canopy_position: float32 [3, 1024, 1024], P(None, 'slab', 'gore'), may hold values from -6 to 6
- tension: float32 [4, 1024, 1024], P(None, 'slab', 'gore'), may hold values from 0.5 to 4
- slot_cut: int32 [1024], replicated, may hold values 0 or 1
- couple_dest: int32 [8, 1024, 2], P('gore', 'slab'), may hold values from 0 to 127, all different within a row; in each aligned block of 64 rows (0 to 63, 64 to 127, ..., all dimensions but the last counted through in order) at most 2 rows name the same one
- couple_block: int32 [8, 1024, 2], P('gore', 'slab'), may hold values from 0 to 2047
- contact_owner: int32 [8, 128, 1], P('gore', 'slab'), may hold values from 0 to 7; in each aligned block of 8 rows (0 to 7, 8 to 15, ..., all dimensions but the last counted through in order) at most 2 rows name the same one
- contact_row: int32 [8, 128], P('gore', 'slab'), may hold values from 0 to 63
Outputs:
- fluid_out: float32 [3, 128, 256, 1024], P(None, 'slab', 'gore')
- canopy_out: float32 [3, 1024, 1024], P(None, 'slab', 'gore')
- contact_force: float32 [16, 8, 16, 3, 128], P('slab', 'gore')
Inputs may be any that keep to these rules, and one draw needn't show every extreme that they name: `couple_dest`: each row names 2 different devices; among the rows of one device no device is named more than 2 times, and some device's rows name one exactly 2 times. `contact_owner`: among the 8 entries of one device no owner is named more than 2 times, and some device names one exactly 2 times.
All inputs are finite; a program needn't handle non-finite values.
Results may differ from a plain program's by a relative error of at most 0.0003.
Values sent between devices are 32-bit elements; how exact they have to be, the bound alone decides.
A program may use at most 128 MiB of HBM per device.

v0:
```python
import math

import jax
import jax.numpy as jnp
from jax import lax
from jax.sharding import PartitionSpec as P

STEPS = 3
SWEEPS = 8


FORCE_SCALE = 0.5
CONTACT_GAIN = 0.1
CONTACT_REACH = 1.0
SOFTEN = 0.01


def with_halo(array, sides, width, wrap):
    for axis, dim in sides:
        peers, length = (lax.axis_size(axis), array.shape[dim])
        up = [(i, (i + 1) % peers) for i in range(peers if wrap else peers - 1)]
        down = [(j, i) for i, j in up]
        last = lax.slice_in_dim(array, length - width, length, axis=dim)
        initial = lax.slice_in_dim(array, 0, width, axis=dim)
        before = lax.ppermute(last, axis, up)
        after = lax.ppermute(initial, axis, down)
        array = jnp.concatenate([before, array, after], axis=dim)
    return array


def pair_force(row_points, row_source, col_points, col_source, col_live):
    differ = row_points[:, :, None] - col_points[:, None, :]
    distance = jnp.sqrt(jnp.sum(differ * differ, axis=0) + SOFTEN)
    spacing = jnp.maximum(CONTACT_REACH - distance, 0.0)
    weight = CONTACT_GAIN * spacing * spacing / distance
    weight = (
        weight
        * (row_source[:, None] != col_source[None, :]).astype(jnp.float32)
        * col_live[None, :]
    )
    return jnp.sum(differ * weight[None], axis=2)


def set_force(points, source, live):
    total_points = points.shape[1]
    block_rows = math.gcd(total_points, 512)
    blocks_count = total_points // block_rows

    def one_block(number):
        begin = number * block_rows
        row_points = lax.dynamic_slice_in_dim(points, begin, block_rows, 1)
        row_source = lax.dynamic_slice_in_dim(source, begin, block_rows, 0)
        row_live = lax.dynamic_slice_in_dim(live, begin, block_rows, 0)
        return pair_force(row_points, row_source, points, source, live) * row_live[None, :]

    pieces = lax.map(one_block, jnp.arange(blocks_count, dtype=jnp.int32))
    return jnp.moveaxis(pieces, 0, 1).reshape(3, total_points)


def route_slots(named, width, capacity):
    onehot = (named[:, None] == jnp.arange(width, dtype=jnp.int32)[None, :]).astype(jnp.int32)
    earlier = jnp.cumsum(onehot, axis=0) - onehot
    ranking = jnp.sum(earlier * onehot, axis=1)
    return named * capacity + ranking


def relax(padded, viscosity):
    center = padded[:, 1:-1, 1:-1]
    sideways = jnp.pad(center, ((0, 0), (0, 0), (0, 0), (1, 1)))
    beside = padded[:, 2:, 1:-1] + padded[:, :-2, 1:-1]
    beside = beside + padded[:, 1:-1, 2:] + padded[:, 1:-1, :-2]
    beside = beside + sideways[..., 2:] + sideways[..., :-2]
    return center + viscosity[None] * (beside - 6.0 * center)


def body(
    fluid_velocity,
    viscosity,
    pressure_jump,
    normals,
    canopy_position,
    tension,
    slot_cut,
    couple_dest,
    couple_block,
    contact_owner,
    contact_row,
):
    slab_count = lax.axis_size("slab")
    gore_count = lax.axis_size("gore")
    device_count = slab_count * gore_count
    planes, y_rows, x_cells = fluid_velocity.shape[1:]
    radial, tile_width = pressure_jump.shape
    coupled = couple_dest.shape[2]
    capacity = max(2, 2 * radial * coupled // device_count)
    line_count = planes * y_rows * (x_cells // tile_width)
    surface = pressure_jump[None] * normals * (1.0 / coupled)
    tiles = jnp.repeat(jnp.moveaxis(surface, 1, 0), coupled, axis=0)
    destination = couple_dest[0].reshape(-1)
    fluid_line = couple_block[0].reshape(-1)
    slot_ids = route_slots(destination, device_count, capacity)
    outgoing = (
        jnp.zeros((device_count * capacity, 3, tile_width), jnp.float32).at[slot_ids].set(tiles)
    )
    aimed = jnp.full((device_count * capacity,), line_count, jnp.int32).at[slot_ids].set(fluid_line)
    arrived, aimed_in = (
        lax.all_to_all(outgoing, ("slab", "gore"), split_axis=0, concat_axis=0, tiled=True),
        lax.all_to_all(aimed, ("slab", "gore"), split_axis=0, concat_axis=0, tiled=True),
    )
    jump_force = (
        jnp.zeros((3, line_count, tile_width), jnp.float32)
        .at[:, aimed_in, :]
        .add(jnp.moveaxis(arrived, 0, 1), mode="drop")
    )
    field = fluid_velocity + FORCE_SCALE * jump_force.reshape(3, planes, y_rows, x_cells)
    for substep in range(STEPS):
        padded = with_halo(field, (("slab", 1), ("gore", 2)), 1, False)
        field = relax(padded, viscosity)
    flat_field = field.reshape(3, line_count, tile_width)
    answer = jnp.moveaxis(jnp.take(flat_field, jnp.minimum(aimed_in, line_count - 1), axis=1), 1, 0)
    returned = lax.all_to_all(answer, ("slab", "gore"), split_axis=0, concat_axis=0, tiled=True)
    sampled = returned[slot_ids].reshape(radial, coupled, 3, tile_width)
    node_velocity = jnp.moveaxis(jnp.sum(sampled, axis=1) * (1.0 / coupled), 1, 0)
    first_row = lax.axis_index("slab") * radial
    keep_down = jnp.concatenate([1 - slot_cut[:-1], jnp.zeros((1,), jnp.int32)]).astype(jnp.float32)
    keep_up = jnp.concatenate([jnp.zeros((1,), jnp.float32), keep_down[:-1]])
    down_here = lax.dynamic_slice_in_dim(keep_down, first_row, radial)
    up_here = lax.dynamic_slice_in_dim(keep_up, first_row, radial)
    w_up = tension[0] * up_here[:, None]
    w_down = tension[1] * down_here[:, None]
    w_left = tension[2]
    w_right = tension[3]
    denominator = 1.0 + w_up + w_down + w_left + w_right
    right_side = canopy_position + node_velocity
    current = canopy_position
    for sweep_number in range(SWEEPS):
        padded = with_halo(current, (("slab", 1), ("gore", 2)), 1, True)
        above = padded[:, :-2, 1:-1]
        below = padded[:, 2:, 1:-1]
        before = padded[:, 1:-1, :-2]
        after = padded[:, 1:-1, 2:]
        current = (
            right_side + w_up * above + w_down * below + w_left * before + w_right * after
        ) / denominator
    owners = contact_owner[0, :, 0]
    picked_rows = contact_row[0]
    listing = owners.shape[0]
    capacity_c = max(2, 2 * listing // gore_count)
    slot_total = gore_count * capacity_c
    chosen = jnp.moveaxis(jnp.take(current, picked_rows, axis=1), 1, 0)
    contact_slots = route_slots(owners, gore_count, capacity_c)
    sending = jnp.zeros((slot_total, 3, tile_width), jnp.float32).at[contact_slots].set(chosen)
    flags = jnp.zeros((slot_total,), jnp.int32).at[contact_slots].set(1)
    gathered, present = (
        lax.all_to_all(
            sending.reshape(gore_count, capacity_c, 3, tile_width),
            "gore",
            split_axis=0,
            concat_axis=0,
            tiled=True,
        ),
        lax.all_to_all(
            flags.reshape(gore_count, capacity_c), "gore", split_axis=0, concat_axis=0, tiled=True
        ),
    )
    tiles_in = gathered.reshape(slot_total, 3, tile_width)
    live_tiles = present.reshape(slot_total)
    points = jnp.moveaxis(tiles_in, 0, 1).reshape(3, slot_total * tile_width)
    tile_source = jnp.arange(slot_total, dtype=jnp.int32) // capacity_c
    source = jnp.repeat(tile_source, tile_width)
    live = jnp.repeat(live_tiles.astype(jnp.float32), tile_width)
    forces = set_force(points, source, live)
    per_slot = jnp.moveaxis(forces.reshape(3, slot_total, tile_width), 0, 1)
    contact_force = per_slot[None, None]
    return (field, current, contact_force)


def solution(mesh):
    in_specs = (
        P(None, "slab", "gore", None),
        P("slab", "gore", None),
        P("slab", "gore"),
        P(None, "slab", "gore"),
        P(None, "slab", "gore"),
        P(None, "slab", "gore"),
        P(),
        P("gore", "slab", None),
        P("gore", "slab", None),
        P("gore", "slab", None),
        P("gore", "slab"),
    )
    out_specs = (
        P(None, "slab", "gore", None),
        P(None, "slab", "gore"),
        P("slab", "gore", None, None, None),
    )
    return jax.shard_map(body, mesh=mesh, in_specs=in_specs, out_specs=out_specs, check_vma=False)
```

profile of v0, /device:TPU:1, one launch (start us, length us, event | category | flops | bytes accessed | tf_op | source)
XLA Modules:
  0.0 362.0 jit_solution(2146319835212246748)
XLA Ops:
  5.6 11.5 %all-to-all-start = ((s32[128,2,1]{1,2,0:T(1,128)}), s32[128,2,1]{1,2,0:T(1,128)S(1)}, u32[]{:S(2)}, u32[]{:S(2)}) async-start(s32[128,2,1]{1,2,0:T(1,128)} %bitcast.2), calls=%async_computation | async-start | bytes 131072 | tf_op jit(solution)/shard_map/all_to_all | solution.py:108
  19.0 13.3 %scatter_fusion = f32[256,3,128]{2,1,0:T(4,128)} fusion(f32[256,3,128]{2,1,0:T(4,128)} %broadcast_in_dim.37, s32[128]{0:T(128)S(1)} %fusion.110, f32[128,3,128]{2,1,0:T(4,128)S(1)} %bitcast.93), kind=kCustom, calls=%fused_computation.4 | custom fusion | bytes 590336 | tf_op jit(solution)/shard_map/scatter | solution.py:103
  32.3 9.8 %all-to-all-start.1 = ((f32[256,3,128]{2,1,0:T(4,128)}), f32[256,3,128]{2,1,0:T(4,128)S(1)}, u32[]{:S(2)}, u32[]{:S(2)}) async-start(f32[256,3,128]{2,1,0:T(4,128)} %scatter_fusion), calls=%async_computation.1 | async-start | bytes 1048576 | tf_op jit(solution)/shard_map/all_to_all | solution.py:107
  44.8 10.8 %all-to-all-done.1 = f32[256,3,128]{2,1,0:T(4,128)S(1)} async-done(((f32[256,3,128]{2,1,0:T(4,128)}), f32[256,3,128]{2,1,0:T(4,128)S(1)}, u32[]{:S(2)}, u32[]{:S(2)}) %all-to-all-start.1) | async-done | bytes 393248 | tf_op jit(solution)/shard_map/all_to_all | solution.py:107
  57.9 24.9 %scatter_fusion.1 = f32[3,2048,128]{2,0,1:T(4,128)} fusion(f32[3,2048,128]{2,0,1:T(4,128)} %broadcast_in_dim.36, s32[256]{0:T(256)S(1)} %bitcast.100, f32[256,3,128]{2,1,0:T(4,128)S(1)} %all-to-all-done.1), kind=kCustom, calls=%fused_computation.5 | custom fusion | flops 98304 | bytes 1180672 | tf_op jit(solution)/shard_map/scatter-add | solution.py:113
  92.6 7.0 %collective-permute-start.1 = (f32[3,1,32,1024]{3,2,1,0:T(8,128)S(1)}, f32[3,1,32,1024]{3,2,1,0:T(8,128)S(1)}, u32[]{:S(2)}, u32[]{:S(2)}) collective-permute-start(f32[3,1,32,1024]{3,2,1,0:T(8,128)S(1)} %get-tuple-element.124), channel_id=1, source_target_pairs={{0,8},{8,16},{16,24},{24,32},{32,40},{40,48},{48,56},{56,64},{64,7... | collective-permute-start | bytes 1179656 | tf_op jit(solution)/shard_map/ppermute | solution.py:25
  99.6 5.0 %collective-permute-done = f32[3,1,32,1024]{3,2,1,0:T(8,128)S(1)} collective-permute-done((f32[3,1,32,1024]{3,2,1,0:T(8,128)S(1)}, f32[3,1,32,1024]{3,2,1,0:T(8,128)S(1)}, u32[]{:S(2)}, u32[]{:S(2)}) %collective-permute-start) | collective-permute-done | bytes 393248 | tf_op jit(solution)/shard_map/ppermute | solution.py:26
  105.8 5.3 %collective-permute-start.2 = (f32[3,10,1,1024]{3,2,1,0:T(1,128)S(1)}, f32[3,10,1,1024]{3,2,1,0:T(1,128)S(1)}, u32[]{:S(2)}, u32[]{:S(2)}) collective-permute-start(f32[3,10,1,1024]{3,2,1,0:T(1,128)S(1)} %get-tuple-element.118), channel_id=1, source_target_pairs={{1,0},{2,1},{3,2},{4,3},{5,4},{6,5},{7,6},{9,8},{10,9},{11,10},{12... | collective-permute-start | bytes 368648 | tf_op jit(solution)/shard_map/ppermute | solution.py:26
  142.6 4.9 %fusion.19 = f32[3,8,32,1024]{3,2,1,0:T(8,128)S(1)} fusion(f32[3,8,32,1024]{3,2,1,0:T(8,128)S(1)} %fusion.14, f32[3,10,1,1024]{3,2,1,0:T(1,128)} %collective-permute-done.7, f32[3,1,32,1024]{3,2,1,0:T(8,128)S(1)} %collective-permute-done.4, f32[3,1,32,1024]{3,2,1,0:T(8,128)} %copy-done.4, f32[3,10,1,1024]{3,2,1,0:T(1,128)} %collective-permute-done.6, ...), kind=kLoop, calls=%fused_computation.39 | loop fusion | flops 13369344 | bytes 8372224 | tf_op jit(solution)/shard_map/add | solution.py:73
  151.7 5.5 %collective-permute-start.9 = (f32[3,1,32,1024]{3,2,1,0:T(8,128)}, f32[3,1,32,1024]{3,2,1,0:T(8,128)}, u32[]{:S(2)}, u32[]{:S(2)}) collective-permute-start(f32[3,1,32,1024]{3,2,1,0:T(8,128)} %get-tuple-element.120), channel_id=1, source_target_pairs={{0,8},{8,16},{16,24},{24,32},{32,40},{40,48},{48,56},{56,64},{64,7... | collective-permute-start | bytes 1179656 | tf_op jit(solution)/shard_map/ppermute | solution.py:25
  167.4 5.5 %collective-permute-start.11 = (f32[3,10,1,1024]{3,2,1,0:T(1,128)S(1)}, f32[3,10,1,1024]{3,2,1,0:T(1,128)S(1)}, u32[]{:S(2)}, u32[]{:S(2)}) collective-permute-start(f32[3,10,1,1024]{3,2,1,0:T(1,128)S(1)} %get-tuple-element.115), channel_id=1, source_target_pairs={{0,1},{1,2},{2,3},{3,4},{4,5},{5,6},{6,7},{8,9},{9,10},{10,11},{11... | collective-permute-start | bytes 368648 | tf_op jit(solution)/shard_map/ppermute | solution.py:25
  174.5 5.9 %fusion.24 = f32[3,8,32,1024]{3,2,1,0:T(8,128)} fusion(f32[3,8,32,1024]{3,2,1,0:T(8,128)S(1)} %copy-done.1, f32[3,10,1,1024]{3,2,1,0:T(1,128)S(1)} %collective-permute-done.11, f32[3,1,32,1024]{3,2,1,0:T(8,128)} %collective-permute-done.8, f32[3,1,32,1024]{3,2,1,0:T(8,128)} %collective-permute-done.9, f32[3,10,1,1024]{3,2,1,0:T(1,128)S(1)} %collective-permute-done.10, ...), kind=kLoop, calls=%fused_computation.44 | loop fusion | flops 13369344 | bytes 8372224 | tf_op jit(solution)/shard_map/add | solution.py:73
  183.2 10.0 %copy.107 = f32[3,2048,128]{2,0,1:T(4,128)} copy(f32[3,2048,128]{2,1,0:T(8,128)S(1)} %reshape.304) | data formatting | bytes 6291456 | tf_op jit(solution)/shard_map/reshape | solution.py:119
  198.3 13.5 %all-to-all-start.2 = ((f32[256,3,128]{2,1,0:T(4,128)}), f32[256,3,128]{2,1,0:T(4,128)S(1)}, u32[]{:S(2)}, u32[]{:S(2)}) async-start(f32[256,3,128]{2,1,0:T(4,128)} %broadcast_select_fusion), calls=%async_computation.2 | async-start | bytes 1048576 | tf_op jit(solution)/shard_map/all_to_all | solution.py:121
  213.9 11.5 %all-to-all-done.2 = f32[256,3,128]{2,1,0:T(4,128)S(1)} async-done(((f32[256,3,128]{2,1,0:T(4,128)}), f32[256,3,128]{2,1,0:T(4,128)S(1)}, u32[]{:S(2)}, u32[]{:S(2)}) %all-to-all-start.2) | async-done | bytes 393248 | tf_op jit(solution)/shard_map/all_to_all | solution.py:121
  240.0 5.1 %collective-permute-start.21 = (f32[3,1,128]{2,0,1:T(4,128)S(1)}, f32[3,1,128]{2,0,1:T(4,128)S(1)}, u32[]{:S(2)}, u32[]{:S(2)}) collective-permute-start(f32[3,1,128]{2,0,1:T(4,128)S(1)} %get-tuple-element.156), channel_id=1, source_target_pairs={{8,0},{16,8},{24,16},{32,24},{40,32},{48,40},{56,48},{64,56},{72,6... | collective-permute-start | bytes 4616 | tf_op jit(solution)/shard_map/ppermute | solution.py:26
  251.6 5.4 %collective-permute-start.25 = (f32[3,1,128]{2,0,1:T(4,128)S(1)}, f32[3,1,128]{2,0,1:T(4,128)S(1)}, u32[]{:S(2)}, u32[]{:S(2)}) collective-permute-start(f32[3,1,128]{2,0,1:T(4,128)S(1)} %get-tuple-element.154), channel_id=1, source_target_pairs={{8,0},{16,8},{24,16},{32,24},{40,32},{48,40},{56,48},{64,56},{72,6... | collective-permute-start | bytes 4616 | tf_op jit(solution)/shard_map/ppermute | solution.py:26
  263.6 5.4 %collective-permute-start.29 = (f32[3,1,128]{2,0,1:T(4,128)S(1)}, f32[3,1,128]{2,0,1:T(4,128)S(1)}, u32[]{:S(2)}, u32[]{:S(2)}) collective-permute-start(f32[3,1,128]{2,0,1:T(4,128)S(1)} %get-tuple-element.152), channel_id=1, source_target_pairs={{8,0},{16,8},{24,16},{32,24},{40,32},{48,40},{56,48},{64,56},{72,6... | collective-permute-start | bytes 4616 | tf_op jit(solution)/shard_map/ppermute | solution.py:26
  276.1 6.1 %all-to-all-start.4 = ((s32[8,1,2]{2,1,0:T(1,128)}), s32[8,1,2]{2,1,0:T(1,128)S(1)}, u32[]{:S(2)}, u32[]{:S(2)}) async-start(s32[8,1,2]{2,1,0:T(1,128)} %bitcast.25), calls=%async_computation.4 | async-start | bytes 8192 | tf_op jit(solution)/shard_map/all_to_all | solution.py:162
  282.6 5.2 %collective-permute-start.33 = (f32[3,1,128]{2,0,1:T(4,128)S(1)}, f32[3,1,128]{2,0,1:T(4,128)S(1)}, u32[]{:S(2)}, u32[]{:S(2)}) collective-permute-start(f32[3,1,128]{2,0,1:T(4,128)S(1)} %get-tuple-element.150), channel_id=1, source_target_pairs={{8,0},{16,8},{24,16},{32,24},{40,32},{48,40},{56,48},{64,56},{72,6... | collective-permute-start | bytes 4616 | tf_op jit(solution)/shard_map/ppermute | solution.py:26
  296.2 5.2 %collective-permute-start.37 = (f32[3,1,128]{2,0,1:T(4,128)S(1)}, f32[3,1,128]{2,0,1:T(4,128)S(1)}, u32[]{:S(2)}, u32[]{:S(2)}) collective-permute-start(f32[3,1,128]{2,0,1:T(4,128)S(1)} %get-tuple-element.148), channel_id=1, source_target_pairs={{8,0},{16,8},{24,16},{32,24},{40,32},{48,40},{56,48},{64,56},{72,6... | collective-permute-start | bytes 4616 | tf_op jit(solution)/shard_map/ppermute | solution.py:26
  308.5 5.2 %collective-permute-start.41 = (f32[3,1,128]{2,0,1:T(4,128)S(1)}, f32[3,1,128]{2,0,1:T(4,128)S(1)}, u32[]{:S(2)}, u32[]{:S(2)}) collective-permute-start(f32[3,1,128]{2,0,1:T(4,128)S(1)} %get-tuple-element.146), channel_id=1, source_target_pairs={{8,0},{16,8},{24,16},{32,24},{40,32},{48,40},{56,48},{64,56},{72,6... | collective-permute-start | bytes 4616 | tf_op jit(solution)/shard_map/ppermute | solution.py:26
  322.1 6.4 %all-to-all-start.3 = ((f32[8,2,3,128]{3,1,2,0:T(2,128)}), f32[8,2,3,128]{3,1,2,0:T(2,128)S(1)}, u32[]{:S(2)}, u32[]{:S(2)}) async-start(f32[8,2,3,128]{3,1,2,0:T(2,128)} %copy.114), calls=%async_computation.3 | async-start | bytes 49152 | tf_op jit(solution)/shard_map/all_to_all | solution.py:155
  333.2 28.2 %while.11 = (s32[]{:T(128)}, f32[4,3,512]{2,1,0:T(4,128)S(1)}, s32[4]{0:T(128)S(1)}, f32[3,2048]{1,0:T(4,128)S(1)}, f32[3,16,128]{2,1,0:T(8,128)S(1)}, /*index=5...) while((s32[]{:T(128)}, f32[4,3,512]{2,1,0:T(4,128)S(1)}, ...), condition=%wide.region_13.14_spmd.clone, body=%wide.region_10.13_spmd.clone.sunk | while | flops 27262980 | bytes 16968008 | solution.py:56
  (261 shorter events, 169.3 us)
Async XLA Ops:
  5.6 26.7 %all-to-all-start = ((s32[128,2,1]{1,2,0:T(1,128)}), s32[128,2,1]{1,2,0:T(1,128)S(1)}, u32[]{:S(2)}, u32[]{:S(2)}) async-start(s32[128,2,1]{1,2,0:T(1,128)} %bitcast.2), calls=%async_computation | async-start | bytes 131072 | tf_op jit(solution)/shard_map/all_to_all | solution.py:108
  32.3 23.3 %all-to-all-start.1 = ((f32[256,3,128]{2,1,0:T(4,128)}), f32[256,3,128]{2,1,0:T(4,128)S(1)}, u32[]{:S(2)}, u32[]{:S(2)}) async-start(f32[256,3,128]{2,1,0:T(4,128)} %scatter_fusion), calls=%async_computation.1 | async-start | bytes 1048576 | tf_op jit(solution)/shard_map/all_to_all | solution.py:107
  91.2 13.5 %collective-permute-start = (f32[3,1,32,1024]{3,2,1,0:T(8,128)S(1)}, f32[3,1,32,1024]{3,2,1,0:T(8,128)S(1)}, u32[]{:S(2)}, u32[]{:S(2)}) collective-permute-start(f32[3,1,32,1024]{3,2,1,0:T(8,128)S(1)} %get-tuple-element.125), channel_id=1, source_target_pairs={{8,0},{16,8},{24,16},{32,24},{40,32},{48,40},{56,48},{64,56},{72,6... | collective-permute-start | bytes 1179656 | tf_op jit(solution)/shard_map/ppermute | solution.py:26
  92.6 13.0 %collective-permute-start.1 = (f32[3,1,32,1024]{3,2,1,0:T(8,128)S(1)}, f32[3,1,32,1024]{3,2,1,0:T(8,128)S(1)}, u32[]{:S(2)}, u32[]{:S(2)}) collective-permute-start(f32[3,1,32,1024]{3,2,1,0:T(8,128)S(1)} %get-tuple-element.124), channel_id=1, source_target_pairs={{0,8},{8,16},{16,24},{24,32},{32,40},{40,48},{48,56},{56,64},{64,7... | collective-permute-start | bytes 1179656 | tf_op jit(solution)/shard_map/ppermute | solution.py:25
  105.8 8.5 %collective-permute-start.2 = (f32[3,10,1,1024]{3,2,1,0:T(1,128)S(1)}, f32[3,10,1,1024]{3,2,1,0:T(1,128)S(1)}, u32[]{:S(2)}, u32[]{:S(2)}) collective-permute-start(f32[3,10,1,1024]{3,2,1,0:T(1,128)S(1)} %get-tuple-element.118), channel_id=1, source_target_pairs={{1,0},{2,1},{3,2},{4,3},{5,4},{6,5},{7,6},{9,8},{10,9},{11,10},{12... | collective-permute-start | bytes 368648 | tf_op jit(solution)/shard_map/ppermute | solution.py:26
  118.7 12.6 %collective-permute-start.4 = (f32[3,1,32,1024]{3,2,1,0:T(8,128)S(1)}, f32[3,1,32,1024]{3,2,1,0:T(8,128)S(1)}, u32[]{:S(2)}, u32[]{:S(2)}) collective-permute-start(f32[3,1,32,1024]{3,2,1,0:T(8,128)S(1)} %get-tuple-element.123), channel_id=1, source_target_pairs={{8,0},{16,8},{24,16},{32,24},{40,32},{48,40},{56,48},{64,56},{72,6... | collective-permute-start | bytes 1179656 | tf_op jit(solution)/shard_map/ppermute | solution.py:26
  120.0 13.1 %collective-permute-start.5 = (f32[3,1,32,1024]{3,2,1,0:T(8,128)S(1)}, f32[3,1,32,1024]{3,2,1,0:T(8,128)S(1)}, u32[]{:S(2)}, u32[]{:S(2)}) collective-permute-start(f32[3,1,32,1024]{3,2,1,0:T(8,128)S(1)} %get-tuple-element.122), channel_id=1, source_target_pairs={{0,8},{8,16},{16,24},{24,32},{32,40},{40,48},{48,56},{56,64},{64,7... | collective-permute-start | bytes 1179656 | tf_op jit(solution)/shard_map/ppermute | solution.py:25
  125.3 47.5 %collective-permute-start.12 = (f32[3,1,128]{2,0,1:T(4,128)}, f32[3,1,128]{2,0,1:T(4,128)S(1)}, u32[]{:S(2)}, u32[]{:S(2)}) collective-permute-start(f32[3,1,128]{2,0,1:T(4,128)} %get-tuple-element.162), channel_id=1, source_target_pairs={{0,8},{8,16},{16,24},{24,32},{32,40},{40,48},{48,56},{56,64},{64,7... | collective-permute-start | bytes 4616 | tf_op jit(solution)/shard_map/ppermute | solution.py:25
  126.8 85.2 %collective-permute-start.13 = (f32[3,1,128]{2,0,1:T(4,128)}, f32[3,1,128]{2,0,1:T(4,128)S(1)}, u32[]{:S(2)}, u32[]{:S(2)}) collective-permute-start(f32[3,1,128]{2,0,1:T(4,128)} %get-tuple-element.161), channel_id=1, source_target_pairs={{8,0},{16,8},{24,16},{32,24},{40,32},{48,40},{56,48},{64,56},{72,6... | collective-permute-start | bytes 4616 | tf_op jit(solution)/shard_map/ppermute | solution.py:26
  134.7 6.7 %collective-permute-start.6 = (f32[3,10,1,1024]{3,2,1,0:T(1,128)}, f32[3,10,1,1024]{3,2,1,0:T(1,128)}, u32[]{:S(2)}, u32[]{:S(2)}) collective-permute-start(f32[3,10,1,1024]{3,2,1,0:T(1,128)} %get-tuple-element.116), channel_id=1, source_target_pairs={{1,0},{2,1},{3,2},{4,3},{5,4},{6,5},{7,6},{9,8},{10,9},{11,10},{12... | collective-permute-start | bytes 368648 | tf_op jit(solution)/shard_map/ppermute | solution.py:26
  150.1 11.8 %collective-permute-start.8 = (f32[3,1,32,1024]{3,2,1,0:T(8,128)}, f32[3,1,32,1024]{3,2,1,0:T(8,128)}, u32[]{:S(2)}, u32[]{:S(2)}) collective-permute-start(f32[3,1,32,1024]{3,2,1,0:T(8,128)} %get-tuple-element.121), channel_id=1, source_target_pairs={{8,0},{16,8},{24,16},{32,24},{40,32},{48,40},{56,48},{64,56},{72,6... | collective-permute-start | bytes 1179656 | tf_op jit(solution)/shard_map/ppermute | solution.py:26
  151.7 12.0 %collective-permute-start.9 = (f32[3,1,32,1024]{3,2,1,0:T(8,128)}, f32[3,1,32,1024]{3,2,1,0:T(8,128)}, u32[]{:S(2)}, u32[]{:S(2)}) collective-permute-start(f32[3,1,32,1024]{3,2,1,0:T(8,128)} %get-tuple-element.120), channel_id=1, source_target_pairs={{0,8},{8,16},{16,24},{24,32},{32,40},{40,48},{48,56},{56,64},{64,7... | collective-permute-start | bytes 1179656 | tf_op jit(solution)/shard_map/ppermute | solution.py:25
  165.4 7.8 %collective-permute-start.10 = (f32[3,10,1,1024]{3,2,1,0:T(1,128)S(1)}, f32[3,10,1,1024]{3,2,1,0:T(1,128)S(1)}, u32[]{:S(2)}, u32[]{:S(2)}) collective-permute-start(f32[3,10,1,1024]{3,2,1,0:T(1,128)S(1)} %get-tuple-element.114), channel_id=1, source_target_pairs={{1,0},{2,1},{3,2},{4,3},{5,4},{6,5},{7,6},{9,8},{10,9},{11,10},{12... | collective-permute-start | bytes 368648 | tf_op jit(solution)/shard_map/ppermute | solution.py:26
  167.4 7.1 %collective-permute-start.11 = (f32[3,10,1,1024]{3,2,1,0:T(1,128)S(1)}, f32[3,10,1,1024]{3,2,1,0:T(1,128)S(1)}, u32[]{:S(2)}, u32[]{:S(2)}) collective-permute-start(f32[3,10,1,1024]{3,2,1,0:T(1,128)S(1)} %get-tuple-element.115), channel_id=1, source_target_pairs={{0,1},{1,2},{2,3},{3,4},{4,5},{5,6},{6,7},{8,9},{9,10},{10,11},{11... | collective-permute-start | bytes 368648 | tf_op jit(solution)/shard_map/ppermute | solution.py:25
  198.3 27.1 %all-to-all-start.2 = ((f32[256,3,128]{2,1,0:T(4,128)}), f32[256,3,128]{2,1,0:T(4,128)S(1)}, u32[]{:S(2)}, u32[]{:S(2)}) async-start(f32[256,3,128]{2,1,0:T(4,128)} %broadcast_select_fusion), calls=%async_computation.2 | async-start | bytes 1048576 | tf_op jit(solution)/shard_map/all_to_all | solution.py:121
  212.1 14.3 %collective-permute-start.14 = (f32[3,66,1]{2,0,1:T(4,128)S(1)}, f32[3,66,1]{2,0,1:T(4,128)S(1)}, u32[]{:S(2)}, u32[]{:S(2)}) collective-permute-start(f32[3,66,1]{2,0,1:T(4,128)S(1)} %get-tuple-element.140), channel_id=1, source_target_pairs={{0,1},{1,2},{2,3},{3,4},{4,5},{5,6},{6,7},{7,0},{8,9},{9,10},{10,1... | collective-permute-start | bytes 2384 | tf_op jit(solution)/shard_map/ppermute | solution.py:25
  213.9 12.5 %collective-permute-start.15 = (f32[3,66,1]{2,0,1:T(4,128)S(1)}, f32[3,66,1]{2,0,1:T(4,128)S(1)}, u32[]{:S(2)}, u32[]{:S(2)}) collective-permute-start(f32[3,66,1]{2,0,1:T(4,128)S(1)} %get-tuple-element.141), channel_id=1, source_target_pairs={{1,0},{2,1},{3,2},{4,3},{5,4},{6,5},{7,6},{0,7},{9,8},{10,9},{11,1... | collective-permute-start | bytes 2384 | tf_op jit(solution)/shard_map/ppermute | solution.py:26
  263.6 6.4 %collective-permute-start.28 = (f32[3,1,128]{2,0,1:T(4,128)S(1)}, f32[3,1,128]{2,0,1:T(4,128)S(1)}, u32[]{:S(2)}, u32[]{:S(2)}) collective-permute-start(f32[3,1,128]{2,0,1:T(4,128)S(1)} %get-tuple-element.151), channel_id=1, source_target_pairs={{0,8},{8,16},{16,24},{24,32},{32,40},{40,48},{48,56},{56,64},{64,7... | collective-permute-start | bytes 4616 | tf_op jit(solution)/shard_map/ppermute | solution.py:25
  270.1 12.1 %collective-permute-start.30 = (f32[3,66,1]{2,0,1:T(4,128)S(1)}, f32[3,66,1]{2,0,1:T(4,128)S(1)}, u32[]{:S(2)}, u32[]{:S(2)}) collective-permute-start(f32[3,66,1]{2,0,1:T(4,128)S(1)} %get-tuple-element.132), channel_id=1, source_target_pairs={{0,1},{1,2},{2,3},{3,4},{4,5},{5,6},{6,7},{7,0},{8,9},{9,10},{10,1... | collective-permute-start | bytes 2384 | tf_op jit(solution)/shard_map/ppermute | solution.py:25
  271.0 11.3 %collective-permute-start.31 = (f32[3,66,1]{2,0,1:T(4,128)S(1)}, f32[3,66,1]{2,0,1:T(4,128)S(1)}, u32[]{:S(2)}, u32[]{:S(2)}) collective-permute-start(f32[3,66,1]{2,0,1:T(4,128)S(1)} %get-tuple-element.133), channel_id=1, source_target_pairs={{1,0},{2,1},{3,2},{4,3},{5,4},{6,5},{7,6},{0,7},{9,8},{10,9},{11,1... | collective-permute-start | bytes 2384 | tf_op jit(solution)/shard_map/ppermute | solution.py:26
  276.1 40.2 %all-to-all-start.4 = ((s32[8,1,2]{2,1,0:T(1,128)}), s32[8,1,2]{2,1,0:T(1,128)S(1)}, u32[]{:S(2)}, u32[]{:S(2)}) async-start(s32[8,1,2]{2,1,0:T(1,128)} %bitcast.25), calls=%async_computation.4 | async-start | bytes 8192 | tf_op jit(solution)/shard_map/all_to_all | solution.py:162
  296.2 6.4 %collective-permute-start.36 = (f32[3,1,128]{2,0,1:T(4,128)S(1)}, f32[3,1,128]{2,0,1:T(4,128)S(1)}, u32[]{:S(2)}, u32[]{:S(2)}) collective-permute-start(f32[3,1,128]{2,0,1:T(4,128)S(1)} %get-tuple-element.147), channel_id=1, source_target_pairs={{0,8},{8,16},{16,24},{24,32},{32,40},{40,48},{48,56},{56,64},{64,7... | collective-permute-start | bytes 4616 | tf_op jit(solution)/shard_map/ppermute | solution.py:25
  296.2 6.3 %collective-permute-start.37 = (f32[3,1,128]{2,0,1:T(4,128)S(1)}, f32[3,1,128]{2,0,1:T(4,128)S(1)}, u32[]{:S(2)}, u32[]{:S(2)}) collective-permute-start(f32[3,1,128]{2,0,1:T(4,128)S(1)} %get-tuple-element.148), channel_id=1, source_target_pairs={{8,0},{16,8},{24,16},{32,24},{40,32},{48,40},{56,48},{64,56},{72,6... | collective-permute-start | bytes 4616 | tf_op jit(solution)/shard_map/ppermute | solution.py:26
  322.1 11.1 %all-to-all-start.3 = ((f32[8,2,3,128]{3,1,2,0:T(2,128)}), f32[8,2,3,128]{3,1,2,0:T(2,128)S(1)}, u32[]{:S(2)}, u32[]{:S(2)}) async-start(f32[8,2,3,128]{3,1,2,0:T(2,128)} %copy.114), calls=%async_computation.3 | async-start | bytes 49152 | tf_op jit(solution)/shard_map/all_to_all | solution.py:155
  (39 other events, 448.5 us)
where the time goes:
time: 364 us; the launch traced here: 362 us
  starting transfers between devices  151 us (41%)
  other arithmetic  79.6 us (22%)
  waiting for transfers between devices  72.7 us (20%)
  local copies, waits for them, and re-layouts  55.1 us (15%)
    ppermute x22, starting transfers between devices, with_halo(): after = lax.ppermute(initial, axis, down)  61.7 us
    ppermute x22, starting transfers between devices, with_halo(): before = lax.ppermute(last, axis, up)  41.5 us
    scatter-add x1, other arithmetic, body(): jump_force = jnp.zeros((3, line_count, tile_width), jnp.float32).at[:, ai...  24.9 us
    ppermute x22, waiting for transfers between devices, with_halo(): after = lax.ppermute(initial, axis, down)  24 us
    ppermute x22, waiting for transfers between devices, with_halo(): before = lax.ppermute(last, axis, up)  22.4 us
    add x3, other arithmetic, relax(): return center + viscosity[None] * (beside - 6.0 * center)  13.9 us
    all_to_all x1, starting transfers between devices, body(): lax.all_to_all(answer, ('slab', 'gore'), split_axis=0, concat_axis=0, til...  13.5 us
    scatter x1, local copies, waits for them, and re-layouts, body(): jnp.zeros((device_count * capacity, 3, tile_width), jnp.float32)  13.3 us
  transfers between devices with their start and end apart: 49, of which 35 were waited for; matrix products, arithmetic and copies ran while one was open for 16% of the time, Pallas kernels for 0%

commit v1 on v0

v1 whole, which is shorter than its diff:
```python
import functools

import jax
import jax.numpy as jnp
from jax import lax
from jax.experimental import pallas as pl
from jax.experimental.pallas import tpu as pltpu
from jax.sharding import PartitionSpec as P

STEPS = 3
SWEEPS = 8
HALO = 8
LANES = 128
GAIN = 0.1
REACH = 1.0
SOFTEN = 0.01
FAR = 1.0e15
MESH = pl.DeviceIdType.MESH
F32 = jnp.float32
BF16 = jnp.bfloat16


def iota(shape, dim):
    return lax.broadcasted_iota(jnp.int32, shape, dim)


def dot(a, b):
    return lax.dot_general(a, b, (((1,), (0,)), ((), ())), preferred_element_type=F32)


def exact_dot(a, b):
    return lax.dot_general(
        a, b, (((1,), (0,)), ((), ())),
        precision=lax.Precision.HIGHEST, preferred_element_type=F32,
    )


def split(x):
    hi = x.astype(BF16)
    return hi, (x - hi.astype(F32)).astype(BF16)


def to_column(row):
    n = row.shape[1]
    same = iota((n, n), 0) == iota((n, n), 1)
    return jnp.sum(jnp.where(same, jnp.broadcast_to(row, (n, n)), 0.0), axis=1, keepdims=True)


def main_kernel(
    slabs, gores,
    fluid_hbm, visc_hbm, jump, normals, canopy, tension, cut, dest, block, owner, picked,
    fluid_out, canopy_out, sets_out,
    v, vis, yh, ys, outbox, inbox, ansbox, retbox, hot_t, hot,
    sc, sl, sr, dc, dl, dr, ext, inv, csend, crecv,
    load_sem, store_sem, zs_sem, zr_sem, ysend_sem, yr_sem, a2a_sem, mem_s, mem_r, con_sem,
):
    s = lax.axis_index("slab")
    g = lax.axis_index("gore")
    me = s * gores + g
    devices = slabs * gores
    cz, cy, nx = vis.shape
    zy = cz * cy
    nbx = nx // LANES
    rows = jump.shape[0]

    def device(t):
        return (lax.div(t, gores), lax.rem(t, gores))

    def rows_of(t, count):
        return pl.ds(pl.multiple_of(t * 8, 8), count)

    loads = [
        pltpu.make_async_copy(fluid_hbm.at[c], v.at[0, c, pl.ds(1, cz)], load_sem.at[c])
        for c in range(3)
    ]
    loads.append(pltpu.make_async_copy(visc_hbm, vis, load_sem.at[3]))
    for copy in loads:
        copy.start()
    barrier = pltpu.get_barrier_semaphore()

    def greet(i, carry):
        t = lax.rem(me + i, devices)
        pl.semaphore_signal(barrier, inc=1, device_id=device(t), device_id_type=MESH)
        return carry

    lax.fori_loop(1, devices, greet, 0)

    zero_plane = jnp.zeros((cy, nx), F32)
    zero_edge = jnp.zeros((cz, nx), F32)

    @pl.when(s == 0)
    def _():
        for step in range(STEPS):
            for c in range(3):
                v[step, c, 0] = zero_plane

    @pl.when(s == slabs - 1)
    def _():
        for step in range(STEPS):
            for c in range(3):
                v[step, c, cz + 1] = zero_plane

    @pl.when(g == 0)
    def _():
        for step in range(STEPS):
            for c in range(3):
                yh[step, 0, c] = zero_edge

    @pl.when(g == gores - 1)
    def _():
        for step in range(STEPS):
            for c in range(3):
                yh[step, 1, c] = zero_edge

    dest_row = jnp.concatenate([dest[0:1, :], dest[1:2, :]], axis=1).astype(F32)
    line_row = jnp.concatenate([block[0:1, :], block[1:2, :]], axis=1).astype(F32)
    entries = 2 * rows
    dest_col = to_column(dest_row)
    line_col = to_column(line_row) + 1.0
    by_dev = (iota((devices, entries), 0).astype(F32) == dest_row).astype(F32)
    by_entry = (iota((entries, devices), 1).astype(F32) == dest_col).astype(F32)
    row_a = lax.rem(iota((entries, entries), 0), rows)
    row_b = lax.rem(iota((entries, entries), 1), rows)
    rank_dev = dot(by_dev.astype(BF16), (row_a < row_b).astype(BF16))
    rank_entry = dot((row_b < row_a).astype(BF16), by_entry.astype(BF16))
    surface = [jump[...] * normals[c] * 0.25 for c in range(3)]
    columns = [jnp.concatenate([t, t], axis=0) for t in surface]
    columns.append(jnp.broadcast_to(line_col, (entries, LANES)))
    table = jnp.concatenate(columns, axis=1)
    lines = []
    for slot in range(2):
        pick = jnp.where(rank_dev == float(slot), by_dev, 0.0)
        placed = exact_dot(pick, table)
        for c in range(3):
            outbox[pl.ds(3 * slot + c, devices, stride=8), :] = placed[:, c * LANES:(c + 1) * LANES]
        lines.append(placed[:, 3 * LANES:])
    outbox[pl.ds(6, devices, stride=8), :] = jnp.where(
        iota((devices, LANES), 1) < LANES // 2, lines[0], lines[1]
    )
    back_pick = jnp.concatenate(
        [jnp.where(rank_entry == float(slot), by_entry, 0.0) for slot in range(2)], axis=1
    ).astype(BF16)

    first = s * rows
    cut_f = cut[...].astype(F32)
    cut_rows, cut_width = cut.shape
    node = first + iota((rows, cut_width), 0)
    lane = iota((rows, cut_width), 1)
    down = jnp.zeros((rows, cut_width), F32)
    up = jnp.zeros((rows, cut_width), F32)
    total_rows = slabs * rows
    for q in range(cut_rows):
        index = q * cut_width + lane
        keep = jnp.broadcast_to(1.0 - cut_f[q:q + 1, :], (rows, cut_width))
        down += jnp.where((index == node) & (index < total_rows - 1), keep, 0.0)
        up += jnp.where(index == node - 1, keep, 0.0)
    keep_down = jnp.sum(down, axis=1, keepdims=True)
    keep_up = jnp.sum(up, axis=1, keepdims=True)
    w_up = tension[0] * keep_up
    w_down = tension[1] * keep_down
    w_left = tension[2]
    w_right = tension[3]
    scale = 1.0 / (1.0 + w_up + w_down + w_left + w_right)
    inv[...] = scale
    own = pl.ds(HALO, rows)
    for i, w in enumerate((w_up, w_down, w_left, w_right)):
        sc[i, own, :] = w * scale
    for c in range(3):
        sc[4 + c, own, :] = canopy[c]

    pl.semaphore_wait(barrier, devices - 1)
    inbox[rows_of(me, 8), :] = outbox[rows_of(me, 8), :]

    def send_all(source, target, count, sem):
        def one(i, carry):
            t = lax.rem(me + i, devices)
            pltpu.make_async_remote_copy(
                source.at[rows_of(t, count)], target.at[rows_of(me, count)],
                a2a_sem.at[sem], a2a_sem.at[sem + 1],
                device_id=device(t), device_id_type=MESH,
            ).start()
            return carry

        lax.fori_loop(1, devices, one, 0)

    def wait_all(buffer, count, sem):
        part = buffer.at[pl.ds(0, (devices - 1) * count)]
        pltpu.make_async_copy(part, part, a2a_sem.at[sem]).wait()

    send_all(outbox, inbox, 7, 0)
    wait_all(inbox, 7, 1)

    def z_copies(step, c):
        up_copy = pltpu.make_async_remote_copy(
            v.at[step, c, cz], v.at[step, c, 0], zs_sem.at[step, 0, c], zr_sem.at[step, 0, c],
            device_id=(lax.rem(s + 1, slabs), g), device_id_type=MESH,
        )
        down_copy = pltpu.make_async_remote_copy(
            v.at[step, c, 1], v.at[step, c, cz + 1], zs_sem.at[step, 1, c], zr_sem.at[step, 1, c],
            device_id=(lax.rem(s + slabs - 1, slabs), g), device_id_type=MESH,
        )
        return up_copy, down_copy

    def y_copies(step, c):
        up_copy = pltpu.make_async_remote_copy(
            ys.at[step, 0, c], yh.at[step, 0, c], ysend_sem.at[step, 0, c], yr_sem.at[step, 0, c],
            device_id=(s, lax.rem(g + 1, gores)), device_id_type=MESH,
        )
        down_copy = pltpu.make_async_remote_copy(
            ys.at[step, 1, c], yh.at[step, 1, c], ysend_sem.at[step, 1, c], yr_sem.at[step, 1, c],
            device_id=(s, lax.rem(g + gores - 1, gores)), device_id_type=MESH,
        )
        return up_copy, down_copy

    def start_pair(pair, at, length):
        @pl.when(at < length - 1)
        def _():
            pair[0].start()

        @pl.when(at > 0)
        def _():
            pair[1].start()

    def recv_pair(pair, at, length):
        @pl.when(at > 0)
        def _():
            pair[0].wait_recv()

        @pl.when(at < length - 1)
        def _():
            pair[1].wait_recv()

    def sent_pair(pair, at, length):
        @pl.when(at < length - 1)
        def _():
            pair[0].wait_send()

        @pl.when(at > 0)
        def _():
            pair[1].wait_send()

    meta = inbox[pl.ds(6, devices, stride=8), :]
    meta_t = meta.T
    line_t = jnp.concatenate(
        [meta_t[0:1, :], meta_t[LANES // 2:LANES // 2 + 1, :]], axis=1
    )
    parts = []
    for c in range(3):
        tiles = jnp.concatenate(
            [inbox[pl.ds(3 * slot + c, devices, stride=8), :] for slot in range(2)], axis=0
        )
        parts.append(split(tiles))
    first_line = (iota((zy, 2 * devices), 0) * nbx + 1).astype(F32)
    for c in range(3):
        loads[c].wait()
        for x in range(nbx):
            if c == 0:
                hot_t[x] = jnp.where(line_t == first_line + float(x), 1.0, 0.0).astype(BF16)
            matrix = hot_t[x]
            added = dot(matrix, parts[c][0]) + dot(matrix, parts[c][1])
            cols = pl.ds(x * LANES, LANES)
            here = v[0, c, pl.ds(1, cz), :, cols]
            v[0, c, pl.ds(1, cz), :, cols] = here + added.reshape(cz, cy, LANES)
        start_pair(z_copies(0, c), s, slabs)
        for z in range(cz):
            ys[0, 0, c, z:z + 1, :] = v[0, c, z + 1, cy - 1:cy, :]
            ys[0, 1, c, z:z + 1, :] = v[0, c, z + 1, 0:1, :]
        start_pair(y_copies(0, c), g, gores)
    loads[3].wait()

    def neighbours(mid, left, right, base):
        below, above = lax.rem(s + 1, slabs), lax.rem(s + slabs - 1, slabs)
        after, before = lax.rem(g + 1, gores), lax.rem(g + gores - 1, gores)
        whole = pl.ds(HALO, rows)
        head = pl.ds(HALO, HALO)
        tail = pl.ds(rows, HALO)
        over = pl.ds(0, HALO)
        under = pl.ds(rows + HALO, HALO)
        plan = (
            (whole, left, whole, (s, after)),
            (whole, right, whole, (s, before)),
            (tail, mid, over, (below, g)),
            (head, mid, under, (above, g)),
            (tail, left, over, (below, after)),
            (tail, right, over, (below, before)),
            (head, left, under, (above, after)),
            (head, right, under, (above, before)),
        )
        return [
            pltpu.make_async_remote_copy(
                mid.at[:, src], to.at[:, dst], mem_s.at[base + i], mem_r.at[base + i],
                device_id=where, device_id_type=MESH,
            )
            for i, (src, to, dst, where) in enumerate(plan)
        ]

    static_halos = neighbours(sc, sl, sr, 0)
    for copy in static_halos:
        copy.start()

    at_line = (iota((devices, zy), 1) * nbx + 1).astype(F32)
    for slot in range(2):
        named = jnp.broadcast_to(
            meta[:, slot * (LANES // 2):slot * (LANES // 2) + 1], (devices, zy)
        )
        for x in range(nbx):
            hot[x, slot * devices:(slot + 1) * devices, :] = jnp.where(
                named == at_line + float(x), 1.0, 0.0
            ).astype(BF16)

    sub = iota((8, nx), 0)
    lan = iota((8, nx), 1)

    def plane(step, c, z, stage):
        blocks = cy // 8
        center = v[step, c, z + 1, pl.ds(0, 8), :]
        up_roll = jnp.broadcast_to(yh[step, 0, c, pl.ds(z, 1), :], (8, nx))
        down_roll = pltpu.roll(center, 7, 0)
        for yb in range(blocks):
            at = pl.ds(8 * yb, 8)
            rolled = pltpu.roll(center, 1, 0)
            upper = jnp.where(sub == 0, up_roll, rolled)
            if yb + 1 < blocks:
                following = v[step, c, z + 1, pl.ds(8 * yb + 8, 8), :]
                next_roll = pltpu.roll(following, 7, 0)
            else:
                following = None
                next_roll = jnp.broadcast_to(yh[step, 1, c, pl.ds(z, 1), :], (8, nx))
            lower = jnp.where(sub == 7, next_roll, down_roll)
            total = v[step, c, z, at, :] + v[step, c, z + 2, at, :]
            total = total + upper + lower
            total = total + jnp.where(lan == 0, 0.0, pltpu.roll(center, 1, 1))
            total = total + jnp.where(lan == nx - 1, 0.0, pltpu.roll(center, nx - 1, 1))
            new = center + vis[z, at, :] * (total - 6.0 * center)
            v[step + 1, c, z + 1, at, :] = new
            if stage and yb == 0:
                ys[step + 1, 1, c, pl.ds(z, 1), :] = new[0:1, :]
            if stage and yb == blocks - 1:
                ys[step + 1, 0, c, pl.ds(z, 1), :] = new[7:8, :]
            center, up_roll, down_roll = following, rolled, next_roll

    def substep(step, c, stage):
        recv_pair(z_copies(step, c), s, slabs)
        recv_pair(y_copies(step, c), g, gores)
        plane(step, c, 0, stage)
        plane(step, c, cz - 1, stage)
        if stage:
            start_pair(z_copies(step + 1, c), s, slabs)

        def inner(z, carry):
            plane(step, c, z, stage)
            return carry

        lax.fori_loop(1, cz - 1, inner, 0)
        if stage:
            start_pair(y_copies(step + 1, c), g, gores)

    def early(i, carry):
        substep(lax.div(i, 3), lax.rem(i, 3), True)
        return carry

    lax.fori_loop(0, 3 * (STEPS - 1), early, 0)

    def last(c, carry):
        substep(STEPS - 1, c, False)
        pltpu.make_async_copy(
            v.at[STEPS, c, pl.ds(1, cz)], fluid_out.at[c], store_sem.at[c]
        ).start()
        sampled = jnp.zeros((2 * devices, LANES), F32)
        for x in range(nbx):
            cell = v[STEPS, c, pl.ds(1, cz), :, pl.ds(x * LANES, LANES)].reshape(zy, LANES)
            hi, lo = split(cell)
            sampled = sampled + dot(hot[x], hi) + dot(hot[x], lo)
        for slot in range(2):
            ansbox[pl.ds(3 * slot + c, devices, stride=8), :] = (
                sampled[slot * devices:(slot + 1) * devices]
            )
        return carry

    lax.fori_loop(0, 3, last, 0)

    retbox[rows_of(me, 8), :] = ansbox[rows_of(me, 8), :]
    send_all(ansbox, retbox, 6, 2)
    wait_all(retbox, 6, 3)
    for c in range(3):
        hi, lo = split(
            jnp.concatenate(
                [retbox[pl.ds(3 * slot + c, devices, stride=8), :] for slot in range(2)], axis=0
            )
        )
        taken = dot(back_pick, hi) + dot(back_pick, lo)
        node_velocity = (taken[:rows] + taken[rows:]) * 0.5
        dc[c, own, :] = (canopy[c] + node_velocity) * inv[...]

    moving_halos = neighbours(dc, dl, dr, 8)
    for copy in moving_halos:
        copy.start()

    wide = iota((rows + 2 * HALO, LANES), 1) < LANES // 2
    for copy in static_halos:
        copy.wait_recv()
    for i in range(7):
        ext[i, :, 0:LANES] = sc[i]
        ext[i, :, LANES:2 * LANES] = jnp.where(wide, sr[i], sl[i])
    for copy in moving_halos:
        copy.wait_recv()
    for c in range(3):
        ext[7 + c, :, 0:LANES] = dc[c]
        ext[7 + c, :, LANES:2 * LANES] = jnp.where(wide, dr[c], dl[c])

    height = rows + 2 * HALO

    def sweep(i, carry):
        for c in range(3):
            p = ext[4 + c]
            new = ext[7 + c] + ext[0] * pltpu.roll(p, 1, 0)
            new = new + ext[1] * pltpu.roll(p, height - 1, 0)
            new = new + ext[2] * pltpu.roll(p, 1, 1)
            new = new + ext[3] * pltpu.roll(p, 2 * LANES - 1, 1)
            ext[4 + c] = new
        return carry

    lax.fori_loop(0, SWEEPS, sweep, 0)

    listed = owner.shape[1]
    owner_f = owner[...].astype(F32)
    picked_col = to_column(picked[...].astype(F32))
    by_owner = (iota((gores, listed), 0).astype(F32) == owner_f).astype(F32)
    before = (iota((listed, listed), 0) < iota((listed, listed), 1)).astype(F32)
    rank = exact_dot(by_owner, before)
    by_row = (iota((listed, rows), 1).astype(F32) == picked_col).astype(F32)
    slots = [jnp.where(rank == float(slot), by_owner, 0.0) for slot in range(2)]
    for c in range(3):
        patch = ext[4 + c, own, 0:LANES]
        canopy_out[c] = patch
        chosen = exact_dot(by_row, patch)
        for slot in range(2):
            csend[pl.ds(3 * slot + c, gores, stride=8), :] = exact_dot(slots[slot], chosen)
    for slot in range(2):
        csend[pl.ds(6 + slot, gores, stride=8), :] = jnp.broadcast_to(
            jnp.sum(slots[slot], axis=1, keepdims=True), (gores, LANES)
        )
    mine = pl.ds(pl.multiple_of(g * 8, 8), 8)
    crecv[mine, :] = csend[mine, :]
    for i in range(1, gores):
        t = lax.rem(g + i, gores)
        pltpu.make_async_remote_copy(
            csend.at[pl.ds(pl.multiple_of(t * 8, 8), 8)], crecv.at[mine],
            con_sem.at[0], con_sem.at[1], device_id=(s, t), device_id_type=MESH,
        ).start()
    most = pl.ds(0, (gores - 1) * 8)
    pltpu.make_async_copy(crecv.at[most], crecv.at[most], con_sem.at[1]).wait()
    sets_out[...] = crecv[...]

    pltpu.make_async_copy(csend.at[most], csend.at[most], con_sem.at[0]).wait()
    wait_all(outbox, 7, 0)
    wait_all(ansbox, 6, 2)
    for copy in static_halos + moving_halos:
        copy.wait_send()

    def drain(i, carry):
        step, c = lax.div(i, 3), lax.rem(i, 3)
        sent_pair(z_copies(step, c), s, slabs)
        sent_pair(y_copies(step, c), g, gores)
        return carry

    lax.fori_loop(0, 3 * STEPS, drain, 0)
    for c in range(3):
        pltpu.make_async_copy(
            v.at[STEPS, c, pl.ds(1, cz)], fluid_out.at[c], store_sem.at[c]
        ).wait()


def contact_kernel(
    gores, fluid_in, canopy_in, sets, fluid_out, canopy_out, force, xj, fj, ft, pad, sem
):
    copies = (
        pltpu.make_async_copy(fluid_in, fluid_out, sem.at[0]),
        pltpu.make_async_copy(canopy_in, canopy_out, sem.at[1]),
    )
    for copy in copies:
        copy.start()
    slots = 2 * gores
    lane = iota((8, LANES), 1)
    pad[...] = jnp.zeros_like(pad)
    for a in range(slots):
        base = (a // 2) * 8
        flag = sets[base + 6 + a % 2:base + 7 + a % 2, :]
        for c in range(3):
            k = c * slots + a
            row = base + 3 * (a % 2) + c
            point = jnp.where(flag > 0.0, sets[row:row + 1, :], FAR)
            pad[k:k + 1, :] = point
            xj[k] = jnp.broadcast_to(point, (8, LANES))
    points_t = pad[...].T
    pad[...] = points_t
    fj[...] = jnp.zeros_like(fj)

    def tile(it, carry):
        at = pl.ds(pl.multiple_of(it * 8, 8), 8)
        column = pad[at, :]
        total = jnp.zeros((8, LANES), F32)
        for a in range(slots - 2):
            xi = [
                jnp.broadcast_to(column[:, c * slots + a:c * slots + a + 1], (8, LANES))
                for c in range(3)
            ]
            acc = [jnp.zeros((8, LANES), F32) for _ in range(3)]
            for b in range(2 * (a // 2) + 2, slots):
                d = [xi[c] - xj[c * slots + b] for c in range(3)]
                square = d[0] * d[0] + d[1] * d[1] + (d[2] * d[2] + SOFTEN)
                inverse = lax.rsqrt(square)
                gap = jnp.maximum(REACH - square * inverse, 0.0)
                weight = gap * gap * inverse
                for c in range(3):
                    push = weight * d[c]
                    acc[c] = acc[c] + push
                    fj[c * slots + b] = fj[c * slots + b] + push
            for c in range(3):
                total = jnp.where(
                    lane == c * slots + a, jnp.sum(acc[c], axis=1, keepdims=True), total
                )
        ft[at, :] = total
        return carry

    lax.fori_loop(0, LANES // 8, tile, 0)
    rows_t = ft[...].T
    for c in range(3):
        for a in range(slots):
            k = c * slots + a
            force[c, a:a + 1, :] = GAIN * (
                rows_t[k:k + 1, :] - jnp.sum(fj[k], axis=0, keepdims=True)
            )
    for copy in copies:
        copy.wait()


def body(
    slabs, gores,
    fluid_velocity, viscosity, pressure_jump, normals, canopy_position, tension,
    slot_cut, couple_dest, couple_block, contact_owner, contact_row,
):
    cz, cy, nx = viscosity.shape
    rows = pressure_jump.shape[0]
    devices = slabs * gores
    zy = cz * cy
    nbx = nx // LANES
    vmem = pl.BlockSpec(memory_space=pltpu.VMEM)
    anywhere = pl.BlockSpec(memory_space=pl.ANY)
    dma = pltpu.SemaphoreType.DMA
    cut_width = min(LANES, slot_cut.shape[0])
    tall = rows + 2 * HALO
    fluid, canopy, sets = pl.pallas_call(
        functools.partial(main_kernel, slabs, gores),
        out_shape=(
            jax.ShapeDtypeStruct(fluid_velocity.shape, F32),
            jax.ShapeDtypeStruct(canopy_position.shape, F32),
            jax.ShapeDtypeStruct((gores * 8, LANES), F32),
        ),
        in_specs=[anywhere, anywhere] + [vmem] * 9,
        out_specs=(anywhere, vmem, vmem),
        scratch_shapes=[
            pltpu.VMEM((STEPS + 1, 3, cz + 2, cy, nx), F32),
            pltpu.VMEM((cz, cy, nx), F32),
            pltpu.VMEM((STEPS, 2, 3, cz, nx), F32),
            pltpu.VMEM((STEPS, 2, 3, cz, nx), F32),
            pltpu.VMEM((devices * 8, LANES), F32),
            pltpu.VMEM((devices * 8, LANES), F32),
            pltpu.VMEM((devices * 8, LANES), F32),
            pltpu.VMEM((devices * 8, LANES), F32),
            pltpu.VMEM((nbx, zy, 2 * devices), BF16),
            pltpu.VMEM((nbx, 2 * devices, zy), BF16),
            pltpu.VMEM((7, tall, LANES), F32),
            pltpu.VMEM((7, tall, LANES), F32),
            pltpu.VMEM((7, tall, LANES), F32),
            pltpu.VMEM((3, tall, LANES), F32),
            pltpu.VMEM((3, tall, LANES), F32),
            pltpu.VMEM((3, tall, LANES), F32),
            pltpu.VMEM((10, tall, 2 * LANES), F32),
            pltpu.VMEM((rows, LANES), F32),
            pltpu.VMEM((gores * 8, LANES), F32),
            pltpu.VMEM((gores * 8, LANES), F32),
            dma((4,)),
            dma((3,)),
            dma((STEPS, 2, 3)),
            dma((STEPS, 2, 3)),
            dma((STEPS, 2, 3)),
            dma((STEPS, 2, 3)),
            dma((4,)),
            dma((16,)),
            dma((16,)),
            dma((2,)),
        ],
        compiler_params=pltpu.CompilerParams(
            collective_id=0, has_side_effects=True, vmem_limit_bytes=56 << 20
        ),
        name="fluid_membrane",
    )(
        fluid_velocity, viscosity, pressure_jump, normals, canopy_position, tension,
        slot_cut.reshape(-1, cut_width),
        couple_dest[0].T, couple_block[0].T, contact_owner[:, :, 0], contact_row,
    )
    slots = 2 * gores
    fluid, canopy, force = pl.pallas_call(
        functools.partial(contact_kernel, gores),
        out_shape=(
            jax.ShapeDtypeStruct(fluid.shape, F32),
            jax.ShapeDtypeStruct(canopy.shape, F32),
            jax.ShapeDtypeStruct((3, slots, LANES), F32),
        ),
        in_specs=[anywhere, anywhere, vmem],
        out_specs=(anywhere, anywhere, vmem),
        scratch_shapes=[
            pltpu.VMEM((3 * slots, 8, LANES), F32),
            pltpu.VMEM((3 * slots, 8, LANES), F32),
            pltpu.VMEM((LANES, LANES), F32),
            pltpu.VMEM((LANES, LANES), F32),
            dma((2,)),
        ],
        name="contact",
    )(fluid, canopy, sets)
    return fluid, canopy, jnp.swapaxes(force, 0, 1)[None, None]


def solution(mesh):
    in_specs = (
        P(None, "slab", "gore", None),
        P("slab", "gore", None),
        P("slab", "gore"),
        P(None, "slab", "gore"),
        P(None, "slab", "gore"),
        P(None, "slab", "gore"),
        P(),
        P("gore", "slab", None),
        P("gore", "slab", None),
        P("gore", "slab", None),
        P("gore", "slab"),
    )
    out_specs = (
        P(None, "slab", "gore", None),
        P(None, "slab", "gore"),
        P("slab", "gore", None, None, None),
    )
    step = functools.partial(body, mesh.shape["slab"], mesh.shape["gore"])
    return jax.shard_map(step, mesh=mesh, in_specs=in_specs, out_specs=out_specs, check_vma=False)
```

time: 364 us -> 176 us (0.48)
  Pallas kernels: 0 us -> 175 us
  starting transfers between devices: 151 us -> 0 us
  other arithmetic: 79.6 us -> 0 us
  waiting for transfers between devices: 72.7 us -> 0 us
  local copies, waits for them, and re-layouts: 55.1 us -> 0 us
    pallas_call x0 -> x2, Pallas kernels: none -> 175 us  [the longest x1 101 us: body(): pl.pallas_call(functools.partial(contact_kernel, gores), out_shape=(jax.S...]
    ppermute x44 -> x0, starting transfers between devices: 103 us -> none  [the longest x22 61.7 us: with_halo(): after = lax.ppermute(initial, axis, down)]
    all_to_all x5 -> x0, starting transfers between devices: 47.3 us -> none  [the longest x1 13.5 us: body(): lax.all_to_all(answer, ('slab', 'gore'), split_axis=0, concat_axis=0, til...]
    ppermute x44 -> x0, waiting for transfers between devices: 46.4 us -> none  [the longest x22 24 us: with_halo(): after = lax.ppermute(initial, axis, down)]
    all_to_all x5 -> x0, waiting for transfers between devices: 26.3 us -> none  [the longest x1 11.5 us: body(): lax.all_to_all(answer, ('slab', 'gore'), split_axis=0, concat_axis=0, til...]
    scatter-add x1 -> x0, other arithmetic: 24.9 us -> none  [body(): jump_force = jnp.zeros((3, line_count, tile_width), jnp.float32).at[:, ai...]
    add x4 -> x0, other arithmetic: 17.4 us -> none  [the longest x3 13.9 us: relax(): return center + viscosity[None] * (beside - 6.0 * center)]
    scatter x4 -> x0, local copies, waits for them, and re-layouts: 15.6 us -> none  [the longest x1 13.3 us: body(): jnp.zeros((device_count * capacity, 3, tile_width), jnp.float32)]
  transfers between devices with their start and end apart: 49 -> 0, of which waited for: 35 -> 0; matrix products, arithmetic and copies ran while one was open for 16% -> 0% of each run, Pallas kernels for 0% -> 0%
where the time goes in v1:
time: 176 us
  Pallas kernels  175 us (99%)
    pallas_call x1, Pallas kernels, body(): pl.pallas_call(functools.partial(contact_kernel, gores), out_shape=(jax.S...  101 us
    pallas_call x1, Pallas kernels, body(): pl.pallas_call(functools.partial(main_kernel, slabs, gores), out_shape=(j...  74.6 us

profile of v1, /device:TPU:1, one launch (start us, length us, event | category | flops | bytes accessed | tf_op | source)
XLA Modules:
  0.0 176.0 jit_solution(10044149173335568285)
XLA Ops:
  0.6 74.6 %fluid_membrane.1 = (f32[3,8,32,1024]{3,2,1,0:T(8,128)}, f32[3,64,128]{2,1,0:T(8,128)}, f32[64,128]{1,0:T(8,128)}) custom-call(f32[3,8,32,1024]{3,2,1,0:T(8,128)} %fluid_hbm.1, f32[8,32,1024]{2,1,0:T(8,128)} %visc_hbm.1, f32[64,128]{1,0:T(8,128)} %jump.1, f32[3,64,128]{2,1,0:T(8,128)} %normals.1, f32[3,64,128]{2,1,0:T(8,128)} %canopy.1, ...), custom_call_target="tpu_custom_call" | custom-call | tf_op jit(solution)/shard_map/fluid_membrane/pallas_call | solution.py:553
  75.2 100.8 %contact.1 = (f32[3,8,32,1024]{3,2,1,0:T(8,128)}, f32[3,64,128]{2,1,0:T(8,128)}, f32[3,16,128]{2,1,0:T(8,128)}) custom-call(f32[3,8,32,1024]{3,2,1,0:T(8,128)} %get-tuple-element.9.fluid_in, f32[3,64,128]{2,1,0:T(8,128)} %get-tuple-element.10.canopy_in, f32[64,128]{1,0:T(8,128)} %get-tuple-element.11.sets), custom_call_target="tpu_custom_call" | custom-call | tf_op jit(solution)/shard_map/contact/pallas_call | solution.py:604

commit v2 on v1

--- a/solution.py
+++ b/solution.py
@@ -472,16 +472,14 @@
 
 
 def contact_kernel(
-    gores, fluid_in, canopy_in, sets, fluid_out, canopy_out, force, xj, fj, ft, pad, sem
+    gores, fluid_in, canopy_in, sets, fluid_out, canopy_out, force, xj, fj, acc_ref, pad, field, sem
 ):
-    copies = (
-        pltpu.make_async_copy(fluid_in, fluid_out, sem.at[0]),
-        pltpu.make_async_copy(canopy_in, canopy_out, sem.at[1]),
-    )
-    for copy in copies:
-        copy.start()
+    load = pltpu.make_async_copy(fluid_in, field, sem.at[0])
+    store = pltpu.make_async_copy(field, fluid_out, sem.at[1])
+    load.start()
+    canopy_out[...] = canopy_in[...]
     slots = 2 * gores
-    lane = iota((8, LANES), 1)
+    group = 8
     pad[...] = jnp.zeros_like(pad)
     for a in range(slots):
         base = (a // 2) * 8
@@ -496,43 +494,55 @@
     pad[...] = points_t
     fj[...] = jnp.zeros_like(fj)
 
-    def tile(it, carry):
-        at = pl.ds(pl.multiple_of(it * 8, 8), 8)
-        column = pad[at, :]
-        total = jnp.zeros((8, LANES), F32)
+    def block(i, carry):
+        at = [pl.ds(pl.multiple_of((i * group + t) * 8, 8), 8) for t in range(group)]
+        column = [pad[rows, :] for rows in at]
         for a in range(slots - 2):
             xi = [
-                jnp.broadcast_to(column[:, c * slots + a:c * slots + a + 1], (8, LANES))
-                for c in range(3)
+                [
+                    jnp.broadcast_to(
+                        column[t][:, c * slots + a:c * slots + a + 1], (8, LANES)
+                    )
+                    for c in range(3)
+                ]
+                for t in range(group)
             ]
-            acc = [jnp.zeros((8, LANES), F32) for _ in range(3)]
+            acc = [[None] * 3 for _ in range(group)]
             for b in range(2 * (a // 2) + 2, slots):
-                d = [xi[c] - xj[c * slots + b] for c in range(3)]
-                square = d[0] * d[0] + d[1] * d[1] + (d[2] * d[2] + SOFTEN)
-                inverse = lax.rsqrt(square)
-                gap = jnp.maximum(REACH - square * inverse, 0.0)
-                weight = gap * gap * inverse
+                other = [xj[c * slots + b] for c in range(3)]
+                pushed = [None] * 3
+                for t in range(group):
+                    d = [xi[t][c] - other[c] for c in range(3)]
+                    square = d[0] * d[0] + d[1] * d[1] + (d[2] * d[2] + SOFTEN)
+                    inverse = lax.rsqrt(square)
+                    gap = jnp.maximum(REACH - square * inverse, 0.0)
+                    weight = gap * gap * inverse
+                    for c in range(3):
+                        push = weight * d[c]
+                        acc[t][c] = push if acc[t][c] is None else acc[t][c] + push
+                        pushed[c] = push if pushed[c] is None else pushed[c] + push
                 for c in range(3):
-                    push = weight * d[c]
-                    acc[c] = acc[c] + push
-                    fj[c * slots + b] = fj[c * slots + b] + push
-            for c in range(3):
-                total = jnp.where(
-                    lane == c * slots + a, jnp.sum(acc[c], axis=1, keepdims=True), total
-                )
-        ft[at, :] = total
+                    fj[c * slots + b] = fj[c * slots + b] + pushed[c]
+            for t in range(group):
+                for c in range(3):
+                    acc_ref[c * slots + a, at[t], :] = acc[t][c]
+
+        @pl.when(i == 0)
+        def _():
+            load.wait()
+            store.start()
+
         return carry
 
-    lax.fori_loop(0, LANES // 8, tile, 0)
-    rows_t = ft[...].T
+    lax.fori_loop(0, LANES // (8 * group), block, 0)
     for c in range(3):
         for a in range(slots):
             k = c * slots + a
-            force[c, a:a + 1, :] = GAIN * (
-                rows_t[k:k + 1, :] - jnp.sum(fj[k], axis=0, keepdims=True)
-            )
-    for copy in copies:
-        copy.wait()
+            total = -jnp.sum(fj[k], axis=0, keepdims=True)
+            if a < slots - 2:
+                total = total + jnp.sum(acc_ref[k].T, axis=0, keepdims=True)
+            force[c, a:a + 1, :] = GAIN * total
+    store.wait()
 
 
 def body(
@@ -608,13 +618,14 @@
             jax.ShapeDtypeStruct(canopy.shape, F32),
             jax.ShapeDtypeStruct((3, slots, LANES), F32),
         ),
-        in_specs=[anywhere, anywhere, vmem],
-        out_specs=(anywhere, anywhere, vmem),
+        in_specs=[anywhere, vmem, vmem],
+        out_specs=(anywhere, vmem, vmem),
         scratch_shapes=[
             pltpu.VMEM((3 * slots, 8, LANES), F32),
             pltpu.VMEM((3 * slots, 8, LANES), F32),
+            pltpu.VMEM((3 * slots, LANES, LANES), F32),
             pltpu.VMEM((LANES, LANES), F32),
-            pltpu.VMEM((LANES, LANES), F32),
+            pltpu.VMEM(fluid.shape, F32),
             dma((2,)),
         ],
         name="contact",

time: 176 us -> 84.1 us (0.48)
  Pallas kernels: 175 us -> 83.3 us
    pallas_call x1, Pallas kernels: 101 us -> 8.65 us  [body(): pl.pallas_call(functools.partial(contact_kernel, gores), out_shape=(jax.S...]
where the time goes in v2:
time: 84.1 us; the launch traced here: 83.9 us
  Pallas kernels  83.3 us (99%)
    pallas_call x1, Pallas kernels, body(): pl.pallas_call(functools.partial(main_kernel, slabs, gores), out_shape=(j...  74.6 us
    pallas_call x1, Pallas kernels, body(): pl.pallas_call(functools.partial(contact_kernel, gores), out_shape=(jax.S...  8.65 us

profile of v2, /device:TPU:1, one launch (start us, length us, event | category | flops | bytes accessed | tf_op | source)
XLA Modules:
  0.0 83.9 jit_solution(15915711720776204172)
XLA Ops:
  0.6 74.6 %fluid_membrane.1 = (f32[3,8,32,1024]{3,2,1,0:T(8,128)}, f32[3,64,128]{2,1,0:T(8,128)}, f32[64,128]{1,0:T(8,128)}) custom-call(f32[3,8,32,1024]{3,2,1,0:T(8,128)} %fluid_hbm.1, f32[8,32,1024]{2,1,0:T(8,128)} %visc_hbm.1, f32[64,128]{1,0:T(8,128)} %jump.1, f32[3,64,128]{2,1,0:T(8,128)} %normals.1, f32[3,64,128]{2,1,0:T(8,128)} %canopy.1, ...), custom_call_target="tpu_custom_call" | custom-call | tf_op jit(solution)/shard_map/fluid_membrane/pallas_call | solution.py:563
  75.2 8.7 %contact.1 = (f32[3,8,32,1024]{3,2,1,0:T(8,128)}, f32[3,64,128]{2,1,0:T(8,128)}, f32[3,16,128]{2,1,0:T(8,128)}) custom-call(f32[3,8,32,1024]{3,2,1,0:T(8,128)} %get-tuple-element.9.fluid_in, f32[3,64,128]{2,1,0:T(8,128)} %get-tuple-element.10.canopy_in, f32[64,128]{1,0:T(8,128)} %get-tuple-element.11.sets), custom_call_target="tpu_custom_call" | custom-call | tf_op jit(solution)/shard_map/contact/pallas_call | solution.py:614

commit v3 on v2

--- a/solution.py
+++ b/solution.py
@@ -48,11 +48,13 @@
 
 def main_kernel(
     slabs, gores,
-    fluid_hbm, visc_hbm, jump, normals, canopy, tension, cut, dest, block, owner, picked,
+    fluid_hbm, visc_hbm, jump_hbm, normals_hbm, canopy_hbm, tension_hbm, cut_hbm,
+    dest_hbm, block_hbm, owner_hbm, picked_hbm,
     fluid_out, canopy_out, sets_out,
+    jump, normals, canopy, tension, cut, dest, block, owner, picked,
     v, vis, yh, ys, outbox, inbox, ansbox, retbox, hot_t, hot,
-    sc, sl, sr, dc, dl, dr, ext, inv, csend, crecv,
-    load_sem, store_sem, zs_sem, zr_sem, ysend_sem, yr_sem, a2a_sem, mem_s, mem_r, con_sem,
+    sc, spr, spl, sl, sr, dc, dpr, dpl, dl, dr, ext, inv, csend, crecv,
+    small_sem, load_sem, store_sem, zs_sem, zr_sem, ysend_sem, yr_sem, a2a_sem, mem_s, mem_r, con_sem,
 ):
     s = lax.axis_index("slab")
     g = lax.axis_index("gore")
@@ -74,7 +76,15 @@
         for c in range(3)
     ]
     loads.append(pltpu.make_async_copy(visc_hbm, vis, load_sem.at[3]))
-    for copy in loads:
+    small = [
+        pltpu.make_async_copy(src, dst, small_sem.at[i])
+        for i, (src, dst) in enumerate((
+            (dest_hbm, dest), (block_hbm, block), (jump_hbm, jump), (normals_hbm, normals),
+            (canopy_hbm, canopy), (tension_hbm, tension), (cut_hbm, cut),
+            (owner_hbm, owner), (picked_hbm, picked),
+        ))
+    ]
+    for copy in small + loads:
         copy.start()
     barrier = pltpu.get_barrier_semaphore()
 
@@ -85,32 +95,8 @@
 
     lax.fori_loop(1, devices, greet, 0)
 
-    zero_plane = jnp.zeros((cy, nx), F32)
-    zero_edge = jnp.zeros((cz, nx), F32)
-
-    @pl.when(s == 0)
-    def _():
-        for step in range(STEPS):
-            for c in range(3):
-                v[step, c, 0] = zero_plane
-
-    @pl.when(s == slabs - 1)
-    def _():
-        for step in range(STEPS):
-            for c in range(3):
-                v[step, c, cz + 1] = zero_plane
-
-    @pl.when(g == 0)
-    def _():
-        for step in range(STEPS):
-            for c in range(3):
-                yh[step, 0, c] = zero_edge
-
-    @pl.when(g == gores - 1)
-    def _():
-        for step in range(STEPS):
-            for c in range(3):
-                yh[step, 1, c] = zero_edge
+    for copy in small:
+        copy.wait()
 
     dest_row = jnp.concatenate([dest[0:1, :], dest[1:2, :]], axis=1).astype(F32)
     line_row = jnp.concatenate([block[0:1, :], block[1:2, :]], axis=1).astype(F32)
@@ -127,19 +113,71 @@
     columns = [jnp.concatenate([t, t], axis=0) for t in surface]
     columns.append(jnp.broadcast_to(line_col, (entries, LANES)))
     table = jnp.concatenate(columns, axis=1)
-    lines = []
+    table_hi, table_lo = split(table)
+    pick = jnp.concatenate(
+        [jnp.where(rank_dev == float(slot), by_dev, 0.0) for slot in range(2)], axis=0
+    ).astype(BF16)
+    placed = dot(pick, table_hi) + dot(pick, table_lo)
     for slot in range(2):
-        pick = jnp.where(rank_dev == float(slot), by_dev, 0.0)
-        placed = exact_dot(pick, table)
         for c in range(3):
-            outbox[pl.ds(3 * slot + c, devices, stride=8), :] = placed[:, c * LANES:(c + 1) * LANES]
-        lines.append(placed[:, 3 * LANES:])
+            outbox[pl.ds(3 * slot + c, devices, stride=8), :] = (
+                placed[slot * devices:(slot + 1) * devices, c * LANES:(c + 1) * LANES]
+            )
     outbox[pl.ds(6, devices, stride=8), :] = jnp.where(
-        iota((devices, LANES), 1) < LANES // 2, lines[0], lines[1]
+        iota((devices, LANES), 1) < LANES // 2,
+        placed[:devices, 3 * LANES:], placed[devices:, 3 * LANES:],
     )
     back_pick = jnp.concatenate(
         [jnp.where(rank_entry == float(slot), by_entry, 0.0) for slot in range(2)], axis=1
     ).astype(BF16)
+
+    pl.semaphore_wait(barrier, devices - 1)
+    inbox[rows_of(me, 8), :] = outbox[rows_of(me, 8), :]
+
+    def send_all(source, target, count, sem):
+        def one(i, carry):
+            t = lax.rem(me + i, devices)
+            pltpu.make_async_remote_copy(
+                source.at[rows_of(t, count)], target.at[rows_of(me, count)],
+                a2a_sem.at[sem], a2a_sem.at[sem + 1],
+                device_id=device(t), device_id_type=MESH,
+            ).start()
+            return carry
+
+        lax.fori_loop(1, devices, one, 0)
+
+    def wait_all(buffer, count, sem):
+        part = buffer.at[pl.ds(0, (devices - 1) * count)]
+        pltpu.make_async_copy(part, part, a2a_sem.at[sem]).wait()
+
+    send_all(outbox, inbox, 7, 0)
+
+    zero_plane = jnp.zeros((cy, nx), F32)
+    zero_edge = jnp.zeros((cz, nx), F32)
+
+    @pl.when(s == 0)
+    def _():
+        for step in range(STEPS):
+            for c in range(3):
+                v[step, c, 0] = zero_plane
+
+    @pl.when(s == slabs - 1)
+    def _():
+        for step in range(STEPS):
+            for c in range(3):
+                v[step, c, cz + 1] = zero_plane
+
+    @pl.when(g == 0)
+    def _():
+        for step in range(STEPS):
+            for c in range(3):
+                yh[step, 0, c] = zero_edge
+
+    @pl.when(g == gores - 1)
+    def _():
+        for step in range(STEPS):
+            for c in range(3):
+                yh[step, 1, c] = zero_edge
 
     first = s * rows
     cut_f = cut[...].astype(F32)
@@ -168,26 +206,6 @@
     for c in range(3):
         sc[4 + c, own, :] = canopy[c]
 
-    pl.semaphore_wait(barrier, devices - 1)
-    inbox[rows_of(me, 8), :] = outbox[rows_of(me, 8), :]
-
-    def send_all(source, target, count, sem):
-        def one(i, carry):
-            t = lax.rem(me + i, devices)
-            pltpu.make_async_remote_copy(
-                source.at[rows_of(t, count)], target.at[rows_of(me, count)],
-                a2a_sem.at[sem], a2a_sem.at[sem + 1],
-                device_id=device(t), device_id_type=MESH,
-            ).start()
-            return carry
-
-        lax.fori_loop(1, devices, one, 0)
-
-    def wait_all(buffer, count, sem):
-        part = buffer.at[pl.ds(0, (devices - 1) * count)]
-        pltpu.make_async_copy(part, part, a2a_sem.at[sem]).wait()
-
-    send_all(outbox, inbox, 7, 0)
     wait_all(inbox, 7, 1)
 
     def z_copies(step, c):
@@ -249,7 +267,7 @@
         tiles = jnp.concatenate(
             [inbox[pl.ds(3 * slot + c, devices, stride=8), :] for slot in range(2)], axis=0
         )
-        parts.append(split(tiles))
+        parts.append(jnp.concatenate(split(tiles), axis=1))
     first_line = (iota((zy, 2 * devices), 0) * nbx + 1).astype(F32)
     for c in range(3):
         loads[c].wait()
@@ -257,7 +275,8 @@
             if c == 0:
                 hot_t[x] = jnp.where(line_t == first_line + float(x), 1.0, 0.0).astype(BF16)
             matrix = hot_t[x]
-            added = dot(matrix, parts[c][0]) + dot(matrix, parts[c][1])
+            added = dot(matrix, parts[c])
+            added = added[:, :LANES] + added[:, LANES:]
             cols = pl.ds(x * LANES, LANES)
             here = v[0, c, pl.ds(1, cz), :, cols]
             v[0, c, pl.ds(1, cz), :, cols] = here + added.reshape(cz, cy, LANES)
@@ -268,35 +287,55 @@
         start_pair(y_copies(0, c), g, gores)
     loads[3].wait()
 
-    def neighbours(mid, left, right, base):
+    def neighbours(mid, to_right, to_left, left, right, base):
         below, above = lax.rem(s + 1, slabs), lax.rem(s + slabs - 1, slabs)
         after, before = lax.rem(g + 1, gores), lax.rem(g + gores - 1, gores)
-        whole = pl.ds(HALO, rows)
-        head = pl.ds(HALO, HALO)
-        tail = pl.ds(rows, HALO)
-        over = pl.ds(0, HALO)
-        under = pl.ds(rows + HALO, HALO)
+        over, under = pl.ds(0, HALO), pl.ds(rows + HALO, HALO)
+        head, tail = pl.ds(0, HALO), pl.ds(rows - HALO, HALO)
         plan = (
-            (whole, left, whole, (s, after)),
-            (whole, right, whole, (s, before)),
-            (tail, mid, over, (below, g)),
-            (head, mid, under, (above, g)),
-            (tail, left, over, (below, after)),
-            (tail, right, over, (below, before)),
-            (head, left, under, (above, after)),
-            (head, right, under, (above, before)),
+            (to_right, left.at[own], (s, after)),
+            (to_left, right.at[own], (s, before)),
+            (mid.at[:, pl.ds(rows, HALO)], mid.at[:, over], (below, g)),
+            (mid.at[:, pl.ds(HALO, HALO)], mid.at[:, under], (above, g)),
+            (to_right.at[tail], left.at[over], (below, after)),
+            (to_left.at[tail], right.at[over], (below, before)),
+            (to_right.at[head], left.at[under], (above, after)),
+            (to_left.at[head], right.at[under], (above, before)),
         )
         return [
             pltpu.make_async_remote_copy(
-                mid.at[:, src], to.at[:, dst], mem_s.at[base + i], mem_r.at[base + i],
+                src, to, mem_s.at[base + i], mem_r.at[base + i],
                 device_id=where, device_id_type=MESH,
             )
-            for i, (src, to, dst, where) in enumerate(plan)
+            for i, (src, to, where) in enumerate(plan)
         ]
 
-    static_halos = neighbours(sc, sl, sr, 0)
-    for copy in static_halos:
-        copy.start()
+    band = lax.div(iota((rows, LANES), 1), HALO)
+
+    def pack(mid, to_right, to_left, count):
+        going_right = jnp.zeros((rows, LANES), F32)
+        going_left = jnp.zeros((rows, LANES), F32)
+        for i in range(count):
+            part = mid[i, own, :]
+            going_right = jnp.where(
+                band == i, pltpu.roll(part, HALO * (i + 1), 1), going_right
+            )
+            moved = part if i == 0 else pltpu.roll(part, HALO * i, 1)
+            going_left = jnp.where(band == i, moved, going_left)
+        to_right[...] = going_right
+        to_left[...] = going_left
+
+    wide = iota((rows + 2 * HALO, LANES), 1)
+
+    def unpack(mid, left, right, i):
+        from_left = pltpu.roll(left[...], LANES - HALO * (i + 1), 1)
+        from_right = right[...] if i == 0 else pltpu.roll(right[...], LANES - HALO * i, 1)
+        side = jnp.where(wide < HALO, from_right, 0.0)
+        side = jnp.where(wide >= LANES - HALO, from_left, side)
+        return mid[i], side
+
+    pack(sc, spr, spl, 7)
+    static_halos = neighbours(sc, spr, spl, sl, sr, 0)
 
     at_line = (iota((devices, zy), 1) * nbx + 1).astype(F32)
     for slot in range(2):
@@ -340,19 +379,18 @@
             center, up_roll, down_roll = following, rolled, next_roll
 
     def substep(step, c, stage):
+        recv_pair(y_copies(step, c), g, gores)
+
+        def inner(z, carry):
+            plane(step, c, z, stage)
+            return carry
+
+        lax.fori_loop(1, cz - 1, inner, 0)
         recv_pair(z_copies(step, c), s, slabs)
-        recv_pair(y_copies(step, c), g, gores)
         plane(step, c, 0, stage)
         plane(step, c, cz - 1, stage)
         if stage:
             start_pair(z_copies(step + 1, c), s, slabs)
-
-        def inner(z, carry):
-            plane(step, c, z, stage)
-            return carry
-
-        lax.fori_loop(1, cz - 1, inner, 0)
-        if stage:
             start_pair(y_copies(step + 1, c), g, gores)
 
     def early(i, carry):
@@ -360,17 +398,19 @@
         return carry
 
     lax.fori_loop(0, 3 * (STEPS - 1), early, 0)
+    for copy in static_halos:
+        copy.start()
 
     def last(c, carry):
         substep(STEPS - 1, c, False)
         pltpu.make_async_copy(
             v.at[STEPS, c, pl.ds(1, cz)], fluid_out.at[c], store_sem.at[c]
         ).start()
-        sampled = jnp.zeros((2 * devices, LANES), F32)
+        sampled = jnp.zeros((2 * devices, 2 * LANES), F32)
         for x in range(nbx):
             cell = v[STEPS, c, pl.ds(1, cz), :, pl.ds(x * LANES, LANES)].reshape(zy, LANES)
-            hi, lo = split(cell)
-            sampled = sampled + dot(hot[x], hi) + dot(hot[x], lo)
+            sampled = sampled + dot(hot[x], jnp.concatenate(split(cell), axis=1))
+        sampled = sampled[:, :LANES] + sampled[:, LANES:]
         for slot in range(2):
             ansbox[pl.ds(3 * slot + c, devices, stride=8), :] = (
                 sampled[slot * devices:(slot + 1) * devices]
@@ -392,21 +432,23 @@
         node_velocity = (taken[:rows] + taken[rows:]) * 0.5
         dc[c, own, :] = (canopy[c] + node_velocity) * inv[...]
 
-    moving_halos = neighbours(dc, dl, dr, 8)
+    pack(dc, dpr, dpl, 3)
+    moving_halos = neighbours(dc, dpr, dpl, dl, dr, 8)
     for copy in moving_halos:
         copy.start()
 
-    wide = iota((rows + 2 * HALO, LANES), 1) < LANES // 2
     for copy in static_halos:
         copy.wait_recv()
     for i in range(7):
-        ext[i, :, 0:LANES] = sc[i]
-        ext[i, :, LANES:2 * LANES] = jnp.where(wide, sr[i], sl[i])
+        middle, side = unpack(sc, sl, sr, i)
+        ext[i, :, 0:LANES] = middle
+        ext[i, :, LANES:2 * LANES] = side
     for copy in moving_halos:
         copy.wait_recv()
     for c in range(3):
-        ext[7 + c, :, 0:LANES] = dc[c]
-        ext[7 + c, :, LANES:2 * LANES] = jnp.where(wide, dr[c], dl[c])
+        middle, side = unpack(dc, dl, dr, c)
+        ext[7 + c, :, 0:LANES] = middle
+        ext[7 + c, :, LANES:2 * LANES] = side
 
     height = rows + 2 * HALO
 
@@ -567,9 +609,18 @@
             jax.ShapeDtypeStruct(canopy_position.shape, F32),
             jax.ShapeDtypeStruct((gores * 8, LANES), F32),
         ),
-        in_specs=[anywhere, anywhere] + [vmem] * 9,
+        in_specs=[anywhere] * 11,
         out_specs=(anywhere, vmem, vmem),
         scratch_shapes=[
+            pltpu.VMEM(pressure_jump.shape, F32),
+            pltpu.VMEM(normals.shape, F32),
+            pltpu.VMEM(canopy_position.shape, F32),
+            pltpu.VMEM(tension.shape, F32),
+            pltpu.VMEM((slot_cut.shape[0] // cut_width, cut_width), jnp.int32),
+            pltpu.VMEM((2, rows), jnp.int32),
+            pltpu.VMEM((2, rows), jnp.int32),
+            pltpu.VMEM(contact_row.shape, jnp.int32),
+            pltpu.VMEM(contact_row.shape, jnp.int32),
             pltpu.VMEM((STEPS + 1, 3, cz + 2, cy, nx), F32),
             pltpu.VMEM((cz, cy, nx), F32),
             pltpu.VMEM((STEPS, 2, 3, cz, nx), F32),
@@ -581,15 +632,20 @@
             pltpu.VMEM((nbx, zy, 2 * devices), BF16),
             pltpu.VMEM((nbx, 2 * devices, zy), BF16),
             pltpu.VMEM((7, tall, LANES), F32),
-            pltpu.VMEM((7, tall, LANES), F32),
-            pltpu.VMEM((7, tall, LANES), F32),
+            pltpu.VMEM((rows, LANES), F32),
+            pltpu.VMEM((rows, LANES), F32),
+            pltpu.VMEM((tall, LANES), F32),
+            pltpu.VMEM((tall, LANES), F32),
             pltpu.VMEM((3, tall, LANES), F32),
-            pltpu.VMEM((3, tall, LANES), F32),
-            pltpu.VMEM((3, tall, LANES), F32),
+            pltpu.VMEM((rows, LANES), F32),
+            pltpu.VMEM((rows, LANES), F32),
+            pltpu.VMEM((tall, LANES), F32),
+            pltpu.VMEM((tall, LANES), F32),
             pltpu.VMEM((10, tall, 2 * LANES), F32),
             pltpu.VMEM((rows, LANES), F32),
             pltpu.VMEM((gores * 8, LANES), F32),
             pltpu.VMEM((gores * 8, LANES), F32),
+            dma((9,)),
             dma((4,)),
             dma((3,)),
             dma((STEPS, 2, 3)),

time: 84.1 us -> 80.1 us (0.952)
  Pallas kernels: 83.3 us -> 79.3 us
    pallas_call x1, Pallas kernels: 74.6 us -> 70.7 us  [body(): pl.pallas_call(functools.partial(main_kernel, slabs, gores), out_shape=(j...]
where the time goes in v3:
time: 80.1 us; the launch traced here: 80 us
  Pallas kernels  79.3 us (99%)
    pallas_call x1, Pallas kernels, body(): pl.pallas_call(functools.partial(main_kernel, slabs, gores), out_shape=(j...  70.7 us
    pallas_call x1, Pallas kernels, body(): pl.pallas_call(functools.partial(contact_kernel, gores), out_shape=(jax.S...  8.65 us

profile of v3, /device:TPU:1, one launch (start us, length us, event | category | flops | bytes accessed | tf_op | source)
XLA Modules:
  0.0 80.0 jit_solution(12604088455037910209)
XLA Ops:
  0.6 70.7 %fluid_membrane.1 = (f32[3,8,32,1024]{3,2,1,0:T(8,128)}, f32[3,64,128]{2,1,0:T(8,128)}, f32[64,128]{1,0:T(8,128)}) custom-call(f32[3,8,32,1024]{3,2,1,0:T(8,128)} %fluid_hbm.1, f32[8,32,1024]{2,1,0:T(8,128)} %visc_hbm.1, f32[64,128]{1,0:T(8,128)} %jump_hbm.1, f32[3,64,128]{2,1,0:T(8,128)} %normals_hbm.1, f32[3,64,128]{2,1,0:T(8,128)} %canopy_hbm.1, ...), custom_call_target="tpu_custom_call" | custom-call | tf_op jit(solution)/shard_map/fluid_membrane/pallas_call | solution.py:605
  71.3 8.7 %contact.1 = (f32[3,8,32,1024]{3,2,1,0:T(8,128)}, f32[3,64,128]{2,1,0:T(8,128)}, f32[3,16,128]{2,1,0:T(8,128)}) custom-call(f32[3,8,32,1024]{3,2,1,0:T(8,128)} %get-tuple-element.9.fluid_in, f32[3,64,128]{2,1,0:T(8,128)} %get-tuple-element.10.canopy_in, f32[64,128]{1,0:T(8,128)} %get-tuple-element.11.sets), custom_call_target="tpu_custom_call" | custom-call | tf_op jit(solution)/shard_map/contact/pallas_call | solution.py:670

commit v4 on v3

--- a/solution.py
+++ b/solution.py
@@ -54,7 +54,7 @@
     jump, normals, canopy, tension, cut, dest, block, owner, picked,
     v, vis, yh, ys, outbox, inbox, ansbox, retbox, hot_t, hot,
     sc, spr, spl, sl, sr, dc, dpr, dpl, dl, dr, ext, inv, csend, crecv,
-    small_sem, load_sem, store_sem, zs_sem, zr_sem, ysend_sem, yr_sem, a2a_sem, mem_s, mem_r, con_sem,
+    small_sem, load_sem, zs_sem, zr_sem, ysend_sem, yr_sem, a2a_sem, mem_s, mem_r, con_sem,
 ):
     s = lax.axis_index("slab")
     g = lax.axis_index("gore")
@@ -371,7 +371,10 @@
             total = total + jnp.where(lan == 0, 0.0, pltpu.roll(center, 1, 1))
             total = total + jnp.where(lan == nx - 1, 0.0, pltpu.roll(center, nx - 1, 1))
             new = center + vis[z, at, :] * (total - 6.0 * center)
-            v[step + 1, c, z + 1, at, :] = new
+            if stage:
+                v[step + 1, c, z + 1, at, :] = new
+            else:
+                fluid_out[c, z, at, :] = new
             if stage and yb == 0:
                 ys[step + 1, 1, c, pl.ds(z, 1), :] = new[0:1, :]
             if stage and yb == blocks - 1:
@@ -403,12 +406,9 @@
 
     def last(c, carry):
         substep(STEPS - 1, c, False)
-        pltpu.make_async_copy(
-            v.at[STEPS, c, pl.ds(1, cz)], fluid_out.at[c], store_sem.at[c]
-        ).start()
         sampled = jnp.zeros((2 * devices, 2 * LANES), F32)
         for x in range(nbx):
-            cell = v[STEPS, c, pl.ds(1, cz), :, pl.ds(x * LANES, LANES)].reshape(zy, LANES)
+            cell = fluid_out[c, :, :, pl.ds(x * LANES, LANES)].reshape(zy, LANES)
             sampled = sampled + dot(hot[x], jnp.concatenate(split(cell), axis=1))
         sampled = sampled[:, :LANES] + sampled[:, LANES:]
         for slot in range(2):
@@ -507,19 +507,17 @@
         return carry
 
     lax.fori_loop(0, 3 * STEPS, drain, 0)
-    for c in range(3):
-        pltpu.make_async_copy(
-            v.at[STEPS, c, pl.ds(1, cz)], fluid_out.at[c], store_sem.at[c]
-        ).wait()
 
 
 def contact_kernel(
-    gores, fluid_in, canopy_in, sets, fluid_out, canopy_out, force, xj, fj, acc_ref, pad, field, sem
+    gores, fluid_in, canopy_in, sets, fluid_out, canopy_out, force, xj, fj, acc_ref, pad, sem
 ):
-    load = pltpu.make_async_copy(fluid_in, field, sem.at[0])
-    store = pltpu.make_async_copy(field, fluid_out, sem.at[1])
-    load.start()
-    canopy_out[...] = canopy_in[...]
+    stores = (
+        pltpu.make_async_copy(fluid_in, fluid_out, sem.at[0]),
+        pltpu.make_async_copy(canopy_in, canopy_out, sem.at[1]),
+    )
+    for store in stores:
+        store.start()
     slots = 2 * gores
     group = 8
     pad[...] = jnp.zeros_like(pad)
@@ -568,12 +566,6 @@
             for t in range(group):
                 for c in range(3):
                     acc_ref[c * slots + a, at[t], :] = acc[t][c]
-
-        @pl.when(i == 0)
-        def _():
-            load.wait()
-            store.start()
-
         return carry
 
     lax.fori_loop(0, LANES // (8 * group), block, 0)
@@ -584,7 +576,8 @@
             if a < slots - 2:
                 total = total + jnp.sum(acc_ref[k].T, axis=0, keepdims=True)
             force[c, a:a + 1, :] = GAIN * total
-    store.wait()
+    for store in stores:
+        store.wait()
 
 
 def body(
@@ -609,8 +602,8 @@
             jax.ShapeDtypeStruct(canopy_position.shape, F32),
             jax.ShapeDtypeStruct((gores * 8, LANES), F32),
         ),
-        in_specs=[anywhere] * 11,
-        out_specs=(anywhere, vmem, vmem),
+        in_specs=[pl.BlockSpec(memory_space=pltpu.HBM)] * 11,
+        out_specs=(vmem, vmem, vmem),
         scratch_shapes=[
             pltpu.VMEM(pressure_jump.shape, F32),
             pltpu.VMEM(normals.shape, F32),
@@ -621,7 +614,7 @@
             pltpu.VMEM((2, rows), jnp.int32),
             pltpu.VMEM(contact_row.shape, jnp.int32),
             pltpu.VMEM(contact_row.shape, jnp.int32),
-            pltpu.VMEM((STEPS + 1, 3, cz + 2, cy, nx), F32),
+            pltpu.VMEM((STEPS, 3, cz + 2, cy, nx), F32),
             pltpu.VMEM((cz, cy, nx), F32),
             pltpu.VMEM((STEPS, 2, 3, cz, nx), F32),
             pltpu.VMEM((STEPS, 2, 3, cz, nx), F32),
@@ -647,7 +640,6 @@
             pltpu.VMEM((gores * 8, LANES), F32),
             dma((9,)),
             dma((4,)),
-            dma((3,)),
             dma((STEPS, 2, 3)),
             dma((STEPS, 2, 3)),
             dma((STEPS, 2, 3)),
@@ -658,14 +650,17 @@
             dma((2,)),
         ],
         compiler_params=pltpu.CompilerParams(
-            collective_id=0, has_side_effects=True, vmem_limit_bytes=56 << 20
+            collective_id=0, has_side_effects=True, vmem_limit_bytes=26 << 20
         ),
         name="fluid_membrane",
-    )(
-        fluid_velocity, viscosity, pressure_jump, normals, canopy_position, tension,
-        slot_cut.reshape(-1, cut_width),
-        couple_dest[0].T, couple_block[0].T, contact_owner[:, :, 0], contact_row,
-    )
+    )(*(
+        pltpu.with_memory_space_constraint(x, pltpu.HBM)
+        for x in (
+            fluid_velocity, viscosity, pressure_jump, normals, canopy_position, tension,
+            slot_cut.reshape(-1, cut_width),
+            couple_dest[0].T, couple_block[0].T, contact_owner[:, :, 0], contact_row,
+        )
+    ))
     slots = 2 * gores
     fluid, canopy, force = pl.pallas_call(
         functools.partial(contact_kernel, gores),
@@ -674,16 +669,16 @@
             jax.ShapeDtypeStruct(canopy.shape, F32),
             jax.ShapeDtypeStruct((3, slots, LANES), F32),
         ),
-        in_specs=[anywhere, vmem, vmem],
-        out_specs=(anywhere, vmem, vmem),
+        in_specs=[vmem, vmem, vmem],
+        out_specs=(anywhere, anywhere, vmem),
         scratch_shapes=[
             pltpu.VMEM((3 * slots, 8, LANES), F32),
             pltpu.VMEM((3 * slots, 8, LANES), F32),
             pltpu.VMEM((3 * slots, LANES, LANES), F32),
             pltpu.VMEM((LANES, LANES), F32),
-            pltpu.VMEM(fluid.shape, F32),
             dma((2,)),
         ],
+        compiler_params=pltpu.CompilerParams(vmem_limit_bytes=12 << 20),
         name="contact",
     )(fluid, canopy, sets)
     return fluid, canopy, jnp.swapaxes(force, 0, 1)[None, None]

time: 80.1 us -> 78.4 us (0.979)
  Pallas kernels: 79.3 us -> 77.7 us
    pallas_call x1, Pallas kernels: 8.65 us -> 7.72 us  [body(): pl.pallas_call(functools.partial(contact_kernel, gores), out_shape=(jax.S...]
where the time goes in v4:
time: 78.4 us; the launch traced here: 78.3 us
  Pallas kernels  77.7 us (99%)
    pallas_call x1, Pallas kernels, body(): pl.pallas_call(functools.partial(main_kernel, slabs, gores), out_shape=(j...  69.9 us
    pallas_call x1, Pallas kernels, body(): pl.pallas_call(functools.partial(contact_kernel, gores), out_shape=(jax.S...  7.72 us

profile of v4, /device:TPU:1, one launch (start us, length us, event | category | flops | bytes accessed | tf_op | source)
XLA Modules:
  0.0 78.3 jit_solution(15481786967062455061)
XLA Ops:
  0.6 69.9 %fluid_membrane.1 = (f32[3,8,32,1024]{3,2,1,0:T(8,128)S(1)}, f32[3,64,128]{2,1,0:T(8,128)S(1)}, f32[64,128]{1,0:T(8,128)S(1)}) custom-call(f32[3,8,32,1024]{3,2,1,0:T(8,128)} %fluid_hbm.1, f32[8,32,1024]{2,1,0:T(8,128)} %visc_hbm.1, f32[64,128]{1,0:T(8,128)} %jump_hbm.1, f32[3,64,128]{2,1,0:T(8,128)} %normals_hbm.1, f32[3,64,128]{2,1,0:T(8,128)} %canopy_hbm.1, ...), custom_call_target="tpu_custom_call" | custom-call | tf_op jit(solution)/shard_map/fluid_membrane/pallas_call | solution.py:598
  70.6 7.7 %contact.1 = (f32[3,8,32,1024]{3,2,1,0:T(8,128)}, f32[3,64,128]{2,1,0:T(8,128)}, f32[3,16,128]{2,1,0:T(8,128)}) custom-call(f32[3,8,32,1024]{3,2,1,0:T(8,128)S(1)} %get-tuple-element.9.fluid_in, f32[3,64,128]{2,1,0:T(8,128)S(1)} %get-tuple-element.10.canopy_in, f32[64,128]{1,0:T(8,128)S(1)} %get-tuple-element.11.sets), custom_call_target="tpu_custom_call" | custom-call | tf_op jit(solution)/shard_map/contact/pallas_call | solution.py:665

commit v5 on v4

--- a/solution.py
+++ b/solution.py
@@ -206,6 +206,20 @@
     for c in range(3):
         sc[4 + c, own, :] = canopy[c]
 
+    listed = owner.shape[1]
+    owner_f = owner[...].astype(F32)
+    picked_col = to_column(picked[...].astype(F32))
+    by_owner = (iota((gores, listed), 0).astype(F32) == owner_f).astype(F32)
+    before = (iota((listed, listed), 0) < iota((listed, listed), 1)).astype(F32)
+    rank = exact_dot(by_owner, before)
+    by_row = (iota((listed, rows), 1).astype(F32) == picked_col).astype(F32)
+    taken_slots = [jnp.where(rank == float(slot), by_owner, 0.0) for slot in range(2)]
+    select = exact_dot(jnp.concatenate(taken_slots, axis=0), by_row).astype(BF16)
+    for slot in range(2):
+        csend[pl.ds(6 + slot, gores, stride=8), :] = jnp.broadcast_to(
+            jnp.sum(taken_slots[slot], axis=1, keepdims=True), (gores, LANES)
+        )
+
     wait_all(inbox, 7, 1)
 
     def z_copies(step, c):
@@ -268,19 +282,37 @@
             [inbox[pl.ds(3 * slot + c, devices, stride=8), :] for slot in range(2)], axis=0
         )
         parts.append(jnp.concatenate(split(tiles), axis=1))
-    first_line = (iota((zy, 2 * devices), 0) * nbx + 1).astype(F32)
+    edge_row = iota((2 * cy, 2 * devices), 0)
+    edge_row = edge_row + jnp.where(edge_row < cy, 0, (cz - 2) * cy)
+    edge_line = (edge_row * nbx + 1).astype(F32)
+    edge_hot = jnp.concatenate(
+        [
+            jnp.where(line_t == edge_line + float(x), 1.0, 0.0).astype(BF16)
+            for x in range(nbx)
+        ],
+        axis=0,
+    )
     for c in range(3):
         loads[c].wait()
+        added = dot(edge_hot, parts[c])
+        added = added[:, :LANES] + added[:, LANES:]
+        for x in range(nbx):
+            cols = pl.ds(x * LANES, LANES)
+            for i, z in enumerate((1, cz)):
+                start = (2 * x + i) * cy
+                v[0, c, z, :, cols] = v[0, c, z, :, cols] + added[start:start + cy]
+        start_pair(z_copies(0, c), s, slabs)
+    inner_rows = (cz - 2) * cy
+    inner_line = ((iota((inner_rows, 2 * devices), 0) + cy) * nbx + 1).astype(F32)
+    for c in range(3):
         for x in range(nbx):
             if c == 0:
-                hot_t[x] = jnp.where(line_t == first_line + float(x), 1.0, 0.0).astype(BF16)
-            matrix = hot_t[x]
-            added = dot(matrix, parts[c])
+                hot_t[x] = jnp.where(line_t == inner_line + float(x), 1.0, 0.0).astype(BF16)
+            added = dot(hot_t[x], parts[c])
             added = added[:, :LANES] + added[:, LANES:]
             cols = pl.ds(x * LANES, LANES)
-            here = v[0, c, pl.ds(1, cz), :, cols]
-            v[0, c, pl.ds(1, cz), :, cols] = here + added.reshape(cz, cy, LANES)
-        start_pair(z_copies(0, c), s, slabs)
+            here = v[0, c, pl.ds(2, cz - 2), :, cols]
+            v[0, c, pl.ds(2, cz - 2), :, cols] = here + added.reshape(cz - 2, cy, LANES)
         for z in range(cz):
             ys[0, 0, c, z:z + 1, :] = v[0, c, z + 1, cy - 1:cy, :]
             ys[0, 1, c, z:z + 1, :] = v[0, c, z + 1, 0:1, :]
@@ -293,14 +325,14 @@
         over, under = pl.ds(0, HALO), pl.ds(rows + HALO, HALO)
         head, tail = pl.ds(0, HALO), pl.ds(rows - HALO, HALO)
         plan = (
-            (to_right, left.at[own], (s, after)),
-            (to_left, right.at[own], (s, before)),
             (mid.at[:, pl.ds(rows, HALO)], mid.at[:, over], (below, g)),
             (mid.at[:, pl.ds(HALO, HALO)], mid.at[:, under], (above, g)),
             (to_right.at[tail], left.at[over], (below, after)),
             (to_left.at[tail], right.at[over], (below, before)),
             (to_right.at[head], left.at[under], (above, after)),
             (to_left.at[head], right.at[under], (above, before)),
+            (to_right, left.at[own], (s, after)),
+            (to_left, right.at[own], (s, before)),
         )
         return [
             pltpu.make_async_remote_copy(
@@ -432,9 +464,11 @@
         node_velocity = (taken[:rows] + taken[rows:]) * 0.5
         dc[c, own, :] = (canopy[c] + node_velocity) * inv[...]
 
+    moving_halos = neighbours(dc, dpr, dpl, dl, dr, 8)
+    for copy in moving_halos[:2]:
+        copy.start()
     pack(dc, dpr, dpl, 3)
-    moving_halos = neighbours(dc, dpr, dpl, dl, dr, 8)
-    for copy in moving_halos:
+    for copy in moving_halos[2:]:
         copy.start()
 
     for copy in static_halos:
@@ -464,24 +498,17 @@
 
     lax.fori_loop(0, SWEEPS, sweep, 0)
 
-    listed = owner.shape[1]
-    owner_f = owner[...].astype(F32)
-    picked_col = to_column(picked[...].astype(F32))
-    by_owner = (iota((gores, listed), 0).astype(F32) == owner_f).astype(F32)
-    before = (iota((listed, listed), 0) < iota((listed, listed), 1)).astype(F32)
-    rank = exact_dot(by_owner, before)
-    by_row = (iota((listed, rows), 1).astype(F32) == picked_col).astype(F32)
-    slots = [jnp.where(rank == float(slot), by_owner, 0.0) for slot in range(2)]
     for c in range(3):
         patch = ext[4 + c, own, 0:LANES]
         canopy_out[c] = patch
-        chosen = exact_dot(by_row, patch)
+        hi, mid = split(patch)
+        low = (patch - hi.astype(F32) - mid.astype(F32)).astype(BF16)
+        chosen = dot(select, jnp.concatenate([hi, mid, low], axis=1))
+        chosen = chosen[:, :LANES] + chosen[:, LANES:2 * LANES] + chosen[:, 2 * LANES:]
         for slot in range(2):
-            csend[pl.ds(3 * slot + c, gores, stride=8), :] = exact_dot(slots[slot], chosen)
-    for slot in range(2):
-        csend[pl.ds(6 + slot, gores, stride=8), :] = jnp.broadcast_to(
-            jnp.sum(slots[slot], axis=1, keepdims=True), (gores, LANES)
-        )
+            csend[pl.ds(3 * slot + c, gores, stride=8), :] = (
+                chosen[slot * gores:(slot + 1) * gores]
+            )
     mine = pl.ds(pl.multiple_of(g * 8, 8), 8)
     crecv[mine, :] = csend[mine, :]
     for i in range(1, gores):
@@ -622,7 +649,7 @@
             pltpu.VMEM((devices * 8, LANES), F32),
             pltpu.VMEM((devices * 8, LANES), F32),
             pltpu.VMEM((devices * 8, LANES), F32),
-            pltpu.VMEM((nbx, zy, 2 * devices), BF16),
+            pltpu.VMEM((nbx, zy - 2 * (zy // cz), 2 * devices), BF16),
             pltpu.VMEM((nbx, 2 * devices, zy), BF16),
             pltpu.VMEM((7, tall, LANES), F32),
             pltpu.VMEM((rows, LANES), F32),

time: 78.4 us -> 77.4 us (0.987)
  Pallas kernels: 77.7 us -> 76.7 us
    pallas_call x1, Pallas kernels: 69.9 us -> 69 us  [body(): pl.pallas_call(functools.partial(main_kernel, slabs, gores), out_shape=(j...]
where the time goes in v5:
time: 77.4 us; the launch traced here: 77.3 us
  Pallas kernels  76.7 us (99%)
    pallas_call x1, Pallas kernels, body(): pl.pallas_call(functools.partial(main_kernel, slabs, gores), out_shape=(j...  69 us
    pallas_call x1, Pallas kernels, body(): pl.pallas_call(functools.partial(contact_kernel, gores), out_shape=(jax.S...  7.72 us

profile of v5, /device:TPU:1, one launch (start us, length us, event | category | flops | bytes accessed | tf_op | source)
XLA Modules:
  0.0 77.3 jit_solution(4812485273226118755)
XLA Ops:
  0.6 69.0 %fluid_membrane.1 = (f32[3,8,32,1024]{3,2,1,0:T(8,128)S(1)}, f32[3,64,128]{2,1,0:T(8,128)S(1)}, f32[64,128]{1,0:T(8,128)S(1)}) custom-call(f32[3,8,32,1024]{3,2,1,0:T(8,128)} %fluid_hbm.1, f32[8,32,1024]{2,1,0:T(8,128)} %visc_hbm.1, f32[64,128]{1,0:T(8,128)} %jump_hbm.1, f32[3,64,128]{2,1,0:T(8,128)} %normals_hbm.1, f32[3,64,128]{2,1,0:T(8,128)} %canopy_hbm.1, ...), custom_call_target="tpu_custom_call" | custom-call | tf_op jit(solution)/shard_map/fluid_membrane/pallas_call | solution.py:625
  69.6 7.7 %contact.1 = (f32[3,8,32,1024]{3,2,1,0:T(8,128)}, f32[3,64,128]{2,1,0:T(8,128)}, f32[3,16,128]{2,1,0:T(8,128)}) custom-call(f32[3,8,32,1024]{3,2,1,0:T(8,128)S(1)} %get-tuple-element.9.fluid_in, f32[3,64,128]{2,1,0:T(8,128)S(1)} %get-tuple-element.10.canopy_in, f32[64,128]{1,0:T(8,128)S(1)} %get-tuple-element.11.sets), custom_call_target="tpu_custom_call" | custom-call | tf_op jit(solution)/shard_map/contact/pallas_call | solution.py:692

commit v6 on v5

--- a/solution.py
+++ b/solution.py
@@ -496,7 +496,7 @@
             ext[4 + c] = new
         return carry
 
-    lax.fori_loop(0, SWEEPS, sweep, 0)
+    lax.fori_loop(0, SWEEPS, sweep, 0, unroll=True)
 
     for c in range(3):
         patch = ext[4 + c, own, 0:LANES]
@@ -546,7 +546,7 @@
     for store in stores:
         store.start()
     slots = 2 * gores
-    group = 8
+    group = 16
     pad[...] = jnp.zeros_like(pad)
     for a in range(slots):
         base = (a // 2) * 8
@@ -705,7 +705,7 @@
             pltpu.VMEM((LANES, LANES), F32),
             dma((2,)),
         ],
-        compiler_params=pltpu.CompilerParams(vmem_limit_bytes=12 << 20),
+        compiler_params=pltpu.CompilerParams(vmem_limit_bytes=28 << 20),
         name="contact",
     )(fluid, canopy, sets)
     return fluid, canopy, jnp.swapaxes(force, 0, 1)[None, None]

time: 77.4 us -> 76.4 us (0.987)
  Pallas kernels: 76.7 us -> 75.7 us
where the time goes in v6:
time: 76.4 us; the launch traced here: 76.3 us
  Pallas kernels  75.7 us (99%)
    pallas_call x1, Pallas kernels, body(): pl.pallas_call(functools.partial(main_kernel, slabs, gores), out_shape=(j...  68.4 us
    pallas_call x1, Pallas kernels, body(): pl.pallas_call(functools.partial(contact_kernel, gores), out_shape=(jax.S...  7.24 us

profile of v6, /device:TPU:1, one launch (start us, length us, event | category | flops | bytes accessed | tf_op | source)
XLA Modules:
  0.0 76.3 jit_solution(10486551488993854353)
XLA Ops:
  0.6 68.4 %fluid_membrane.1 = (f32[3,8,32,1024]{3,2,1,0:T(8,128)S(1)}, f32[3,64,128]{2,1,0:T(8,128)S(1)}, f32[64,128]{1,0:T(8,128)S(1)}) custom-call(f32[3,8,32,1024]{3,2,1,0:T(8,128)} %fluid_hbm.1, f32[8,32,1024]{2,1,0:T(8,128)} %visc_hbm.1, f32[64,128]{1,0:T(8,128)} %jump_hbm.1, f32[3,64,128]{2,1,0:T(8,128)} %normals_hbm.1, f32[3,64,128]{2,1,0:T(8,128)} %canopy_hbm.1, ...), custom_call_target="tpu_custom_call" | custom-call | tf_op jit(solution)/shard_map/fluid_membrane/pallas_call | solution.py:625
  69.1 7.2 %contact.1 = (f32[3,8,32,1024]{3,2,1,0:T(8,128)}, f32[3,64,128]{2,1,0:T(8,128)}, f32[3,16,128]{2,1,0:T(8,128)}) custom-call(f32[3,8,32,1024]{3,2,1,0:T(8,128)S(1)} %get-tuple-element.9.fluid_in, f32[3,64,128]{2,1,0:T(8,128)S(1)} %get-tuple-element.10.canopy_in, f32[64,128]{1,0:T(8,128)S(1)} %get-tuple-element.11.sets), custom_call_target="tpu_custom_call" | custom-call | tf_op jit(solution)/shard_map/contact/pallas_call | solution.py:692
